TPU v7x, 128 devices: a whole 4x4x4 slice. The times are simulated.
128 devices in a mesh: row: 16 (over x, z), col: 8 (over y, core).
Axes of the slice: x: 4, y: 4, z: 4, core: 2. Of those that a mesh axis runs over, the one named last changes fastest.
Arguments:
- tiles: bfloat16 [768, 1024, 1024], P(('row', 'col')), may hold values from -0.1875 to 0.1875
- tile_list: int32 [768, 2], P(('row', 'col')), may hold values from 0 to 63, as said below
- tile_count: int32 [128], P(('row', 'col')), may hold values from 1 to 6, as said below
- scale_index: int32 [768], P(('row', 'col')), may hold values from 0 to 63
- scales: float32 [64], replicated, may hold values from 0.25 to 4
- panel_start: bfloat16 [65536, 128], P(('row', 'col')), may hold values from -6 to 6
- centroids: bfloat16 [4096, 128], replicated, may hold values from -2 to 2
Outputs:
- panel: bfloat16 [65536, 128], P(('row', 'col'))
- centers: float32 [4096, 128], replicated
Inputs may be any that keep to these rules, and one draw needn't show every extreme that they name: `tile_list`: device d holds slots d * 6 to (d + 1) * 6 - 1. With d = i * 8 + j, its tiles lie in row blocks i * 4 to (i + 1) * 4 - 1 and column blocks j * 8 to (j + 1) * 8 - 1, and no two slots of a device name the same block. `tile_count`: live slots of each device; some device fills all its slots.
All inputs are finite; a program needn't handle non-finite values.
Results may differ from a plain program's by a relative error of at most 0.008.
Values may be sent and summed in bfloat16 or wider, within the bound.
No kernel may reach another device: no remote copies, remote signals or barrier semaphores. Data moves between devices by JAX's collectives and lax.ppermute only.
A program may use at most 128 MiB of HBM per device.

v0:
```python
import jax
import jax.numpy as jnp
from jax import lax
from jax.sharding import PartitionSpec as P

ROUNDS = 2


SHARPNESS = 48.0
EPS = 1e-06


def accumulate(
    tiles, source_blocks, target_blocks, weights, live_count, gathered, out_rows, transposed
):
    block_size = tiles.shape[1]

    def add_tile(slot_index, running):
        tile_data = lax.dynamic_index_in_dim(tiles, slot_index, 0, keepdims=False)
        source_rows = lax.dynamic_slice_in_dim(
            gathered, source_blocks[slot_index] * block_size, block_size, 0
        )
        if transposed:
            product_block = lax.dot_general(
                tile_data, source_rows, (((0,), (0,)), ((), ())), preferred_element_type=jnp.float32
            )
        else:
            product_block = jnp.dot(tile_data, source_rows, preferred_element_type=jnp.float32)
        offset = target_blocks[slot_index] * block_size
        current = lax.dynamic_slice_in_dim(running, offset, block_size, 0)
        return lax.dynamic_update_slice_in_dim(
            running, current + weights[slot_index] * product_block, offset, 0
        )

    start_sum = jnp.zeros((out_rows, gathered.shape[1]), jnp.float32)
    return lax.fori_loop(0, live_count, add_tile, start_sum)


def local_gram(product):
    return lax.dot_general(
        product,
        product,
        (((0,), (0,)), ((), ())),
        precision=lax.Precision.HIGHEST,
        preferred_element_type=jnp.float32,
    )


def finish(product, gram_matrix):
    lower_factor = jnp.linalg.cholesky(gram_matrix)
    identity = jnp.eye(product.shape[1], dtype=jnp.float32)
    inverse = lax.linalg.triangular_solve(lower_factor, identity, left_side=True, lower=True)
    return jnp.dot(
        product, inverse.T, precision=lax.Precision.HIGHEST, preferred_element_type=jnp.float32
    ).astype(jnp.bfloat16)


def orthonormal(product, total_rows):
    gram_matrix = lax.psum(local_gram(product), ("row", "col")) / total_rows
    return finish(product, gram_matrix)


def shards(tiles, tile_list, tile_count, scale_index, scales, panel_start, centroids):
    block_size = tiles.shape[1]
    piece_rows = panel_start.shape[0]
    rows_axis = lax.axis_size("row")
    cols_axis = lax.axis_size("col")
    total_rows = piece_rows * rows_axis * cols_axis
    row_at = lax.axis_index("row")
    col_at = lax.axis_index("col")
    range_rows = piece_rows * cols_axis
    range_cols = piece_rows * rows_axis
    local_rows = tile_list[:, 0] - row_at * (range_rows // block_size)
    local_cols = tile_list[:, 1] - col_at * (range_cols // block_size)
    live_count = tile_count[0]
    table_ids = jnp.arange(scales.shape[0], dtype=jnp.int32)
    weights = jnp.sum(
        jnp.where(scale_index[:, None] == table_ids[None, :], scales[None, :], 0.0), axis=1
    )
    panel = panel_start
    for round_index in range(ROUNDS):
        gathered = lax.all_gather(panel, "col", axis=0, tiled=True)
        partial_sum = accumulate(
            tiles, local_rows, local_cols, weights, live_count, gathered, range_cols, True
        )
        product = lax.psum_scatter(partial_sum, "row", scatter_dimension=0, tiled=True)
        factor = orthonormal(product, total_rows)
        gathered = lax.all_gather(factor, "row", axis=0, tiled=True)
        partial_sum = accumulate(
            tiles, local_cols, local_rows, weights, live_count, gathered, range_rows, False
        )
        product = lax.psum_scatter(partial_sum, "col", scatter_dimension=0, tiled=True)
        panel = orthonormal(product, total_rows)
    values = panel.astype(jnp.float32)
    row_norm = jnp.sqrt(jnp.sum(values * values, axis=1, keepdims=True) + EPS)
    points = (values / row_norm).astype(jnp.bfloat16)
    center_values = centroids.astype(jnp.float32)
    center_sq = jnp.sum(center_values * center_values, axis=1)
    affinity = lax.dot_general(
        points, centroids, (((1,), (1,)), ((), ())), preferred_element_type=jnp.float32
    )
    scores = SHARPNESS * (2.0 * affinity - center_sq[None, :])
    shifted = jnp.exp(scores - jnp.max(scores, axis=1, keepdims=True))
    resp = (shifted / jnp.sum(shifted, axis=1, keepdims=True)).astype(jnp.bfloat16)
    sums = lax.dot_general(
        resp, points, (((0,), (0,)), ((), ())), preferred_element_type=jnp.float32
    )
    totals = jnp.sum(resp.astype(jnp.float32), axis=0)
    all_sums, all_totals = lax.psum((sums, totals), ("row", "col"))
    centers = (all_sums + center_values) / (all_totals[:, None] + 1.0)
    return (panel, centers)


def solution(mesh):
    return jax.shard_map(
        shards,
        mesh=mesh,
        in_specs=(
            P(("row", "col"), None, None),
            P(("row", "col"), None),
            P(("row", "col")),
            P(("row", "col")),
            P(),
            P(("row", "col"), None),
            P(),
        ),
        out_specs=(P(("row", "col"), None), P()),
        check_vma=False,
    )
```

profile of v0, /device:TPU:0, one launch (start us, length us, event | category | flops | bytes accessed | tf_op | source)
XLA Modules:
  0.0 1388.8 jit_solution(2792760650536709020)
XLA Ops:
  9.6 25.9 %all-gather.5.cloned.1.call-done = bf16[4096,128]{1,0:T(8,128)(2,1)} async-done(((bf16[512,128]{1,0:T(8,128)(2,1)}), bf16[4096,128]{1,0:T(8,128)(2,1)}) %all-gather.5.cloned.1.call-update) | async-done | bytes 1048592 | tf_op jit(solution)/shard_map/all_gather | solution.py:82
  35.5 2.2 broadcast.62.clone
  37.7 16.0 %while.40 = (s32[]{:T(128)}, f32[8192,128]{1,0:T(8,128)}, s32[]{:T(128)}, s32[6]{0:T(128)S(1)}, f32[6]{0:T(128)S(1)}, /*index=5*/bf16[6,1024,1024]{2,1,0:T(8,128...) while((s32[]{:T(128)}, f32[8192,128]{1,0:T(8,128)}, ...), condition=%wide.region_2.3_spmd, body=%wide.region_1.2_spmd.sunk | while | flops 268697600 | bytes 3408691 | solution.py:36
  41.4 3.9 fusion.121
  49.1 4.0 fusion.121
  53.8 107.0 %reduce-scatter.5.cloned.1.call-done = f32[512,128]{1,0:T(8,128)} async-done(((f32[8192,128]{1,0:T(8,128)}), f32[512,128]{1,0:T(8,128)}) %reduce-scatter.5.cloned.1.call-update) | async-done | bytes 262160 | tf_op jit(solution)/shard_map/reduce_scatter | solution.py:86
  160.8 2.2 fusion.85
  163.1 139.3 %all-reduce.6.cloned.1.call-done = f32[128,128]{0,1:T(8,128)} async-done(((f32[128,128]{0,1:T(8,128)}), f32[128,128]{0,1:T(8,128)}) %all-reduce.6.cloned.1.call-update) | async-done | bytes 65552 | tf_op jit(solution)/shard_map/psum | solution.py:59
  304.2 11.7 cholesky.74
  317.3 9.8 custom-call.8
  327.4 2.0 convolution_convert_fusion.3
  329.5 44.5 %all-gather.7.cloned.1.call-done = bf16[8192,128]{1,0:T(8,128)(2,1)} async-done(((bf16[512,128]{1,0:T(8,128)(2,1)}), bf16[8192,128]{1,0:T(8,128)(2,1)}) %all-gather.7.cloned.1.call-update) | async-done | bytes 2097168 | tf_op jit(solution)/shard_map/all_gather | solution.py:88
  374.1 14.1 %while.41 = (s32[]{:T(128)}, f32[4096,128]{1,0:T(8,128)S(1)}, s32[]{:T(128)}, s32[6]{0:T(128)S(1)}, f32[6]{0:T(128)S(1)}, /*index=5*/bf16[6,1024,1024]{2,1,0:T(8...) while((s32[]{:T(128)}, f32[4096,128]{1,0:T(8,128)S(1)}, ...), condition=%wide.region_8.11_spmd, body=%wide.region_7.10_spmd.sunk | while | flops 268697600 | bytes 3408691 | solution.py:36
  377.9 3.0 fusion.124
  384.6 3.0 fusion.124
  389.6 59.0 %reduce-scatter.7.cloned.1.call-done = f32[512,128]{1,0:T(8,128)} async-done(((f32[4096,128]{1,0:T(8,128)}), f32[512,128]{1,0:T(8,128)}) %reduce-scatter.7.cloned.1.call-update) | async-done | bytes 262160 | tf_op jit(solution)/shard_map/reduce_scatter | solution.py:92
  448.6 2.2 fusion.86
  451.5 138.3 %all-reduce.8.cloned.1.call-done = f32[128,128]{0,1:T(8,128)} async-done(((f32[128,128]{0,1:T(8,128)}), f32[128,128]{0,1:T(8,128)}) %all-reduce.8.cloned.1.call-update) | async-done | bytes 65552 | tf_op jit(solution)/shard_map/psum | solution.py:59
  591.6 11.7 cholesky.85
  604.7 9.8 custom-call.9
  614.8 2.0 convolution_convert_fusion.2
  616.8 22.8 %all-gather.9.cloned.1.call-done = bf16[4096,128]{1,0:T(8,128)(2,1)} async-done(((bf16[512,128]{1,0:T(8,128)(2,1)}), bf16[4096,128]{1,0:T(8,128)(2,1)}) %all-gather.9.cloned.1.call-update) | async-done | bytes 1048592 | tf_op jit(solution)/shard_map/all_gather | solution.py:82
  639.6 2.2 broadcast.62
  641.8 16.0 %while.42 = (s32[]{:T(128)}, f32[8192,128]{1,0:T(8,128)}, s32[]{:T(128)}, s32[6]{0:T(128)S(1)}, f32[6]{0:T(128)S(1)}, /*index=5*/bf16[6,1024,1024]{2,1,0:T(8,128...) while((s32[]{:T(128)}, f32[8192,128]{1,0:T(8,128)}, ...), condition=%wide.region_12.15_spmd, body=%wide.region_11.14_spmd.sunk | while | flops 268697600 | bytes 3408691 | solution.py:36
  645.5 3.9 fusion.127
  653.2 4.0 fusion.127
  657.9 107.0 %reduce-scatter.9.cloned.1.call-done = f32[512,128]{1,0:T(8,128)} async-done(((f32[8192,128]{1,0:T(8,128)}), f32[512,128]{1,0:T(8,128)}) %reduce-scatter.9.cloned.1.call-update) | async-done | bytes 262160 | tf_op jit(solution)/shard_map/reduce_scatter | solution.py:86
  764.9 2.2 fusion.87
  767.4 139.1 %all-reduce.10.cloned.1.call-done = f32[128,128]{0,1:T(8,128)} async-done(((f32[128,128]{0,1:T(8,128)}), f32[128,128]{0,1:T(8,128)}) %all-reduce.10.cloned.1.call-update) | async-done | bytes 65552 | tf_op jit(solution)/shard_map/psum | solution.py:59
  908.4 11.7 cholesky.96
  921.4 9.8 custom-call.10
  931.5 2.0 convolution_convert_fusion.1
  933.6 44.5 %all-gather.11.cloned.1.call-done = bf16[8192,128]{1,0:T(8,128)(2,1)} async-done(((bf16[512,128]{1,0:T(8,128)(2,1)}), bf16[8192,128]{1,0:T(8,128)(2,1)}) %all-gather.11.cloned.1.call-update) | async-done | bytes 2097168 | tf_op jit(solution)/shard_map/all_gather | solution.py:88
  978.3 14.2 %while.43 = (s32[]{:T(128)}, f32[4096,128]{1,0:T(8,128)S(1)}, s32[]{:T(128)}, s32[6]{0:T(128)S(1)}, f32[6]{0:T(128)S(1)}, /*index=5*/bf16[6,1024,1024]{2,1,0:T(8...) while((s32[]{:T(128)}, f32[4096,128]{1,0:T(8,128)S(1)}, ...), condition=%wide.region_16.19_spmd, body=%wide.region_15.18_spmd.sunk | while | flops 268697600 | bytes 3408691 | solution.py:36
  982.1 3.0 fusion.130
  988.8 3.0 fusion.130
  993.9 59.0 %reduce-scatter.11.cloned.1.call-done = f32[512,128]{1,0:T(8,128)} async-done(((f32[4096,128]{1,0:T(8,128)}), f32[512,128]{1,0:T(8,128)}) %reduce-scatter.11.cloned.1.call-update) | async-done | bytes 262160 | tf_op jit(solution)/shard_map/reduce_scatter | solution.py:92
  1052.8 2.2 fusion.88
  1056.0 138.1 %all-reduce.12.cloned.1.call-done = f32[128,128]{0,1:T(8,128)} async-done(((f32[128,128]{0,1:T(8,128)}), f32[128,128]{0,1:T(8,128)}) %all-reduce.12.cloned.1.call-update) | async-done | bytes 65552 | tf_op jit(solution)/shard_map/psum | solution.py:59
  1195.9 11.7 cholesky.107
  1208.9 9.8 custom-call.11
  1219.0 1.4 fusion.59
  1220.4 1.4 fusion.84
  1223.1 2.4 convert_reduce_fusion
  1225.5 2.6 fusion.81
  1228.8 66.9 %psum.47 = f32[4096]{0:T(1024)S(1)} all-reduce(f32[4096]{0:T(1024)S(1)} %get-tuple-element.248), channel_id=1, replica_groups=mesh['row'=16,'col'=8] {'row','col'}, use_global_device_ids=true, to_apply=%region_25.28 | all-reduce | flops 4096 | bytes 32768 | tf_op jit(solution)/shard_map/psum | solution.py:109
  1295.7 83.4 %all-reduce.14.cloned.1.call-done = f32[4096,128]{1,0:T(8,128)} async-done(((f32[4096,128]{1,0:T(8,128)}), f32[4096,128]{1,0:T(8,128)}) %all-reduce.14.cloned.1.call-update) | async-done | bytes 2097168 | tf_op jit(solution)/shard_map/psum | solution.py:109
  1379.1 2.9 fusion.58
  (93 shorter events, 37.3 us)
Async XLA Ops:
  7.2 28.3 %all-gather.5.cloned.1.call-start = ((), (), s32[]{:S(2)}) async-start(), calls=%async_computation.4 | async-start | bytes 1179648 | tf_op jit(solution)/shard_map/all_gather | solution.py:82
  7.9 152.9 %reduce-scatter.5.cloned.1.call-start = ((), (), s32[]{:S(2)}) async-start(), calls=%async_computation.5 | async-start | bytes 4456448 | tf_op jit(solution)/shard_map/reduce_scatter | solution.py:86
  53.7 248.7 %all-reduce.6.cloned.1.call-start = ((), (), s32[]{:S(2)}) async-start(), calls=%async_computation.6 | async-start | bytes 131072 | tf_op jit(solution)/shard_map/psum | solution.py:59
  163.1 210.9 %all-gather.7.cloned.1.call-start = ((), (), s32[]{:S(2)}) async-start(), calls=%async_computation.7 | async-start | bytes 2228224 | tf_op jit(solution)/shard_map/all_gather | solution.py:88
  329.4 119.2 %reduce-scatter.7.cloned.1.call-start = ((), (), s32[]{:S(2)}) async-start(), calls=%async_computation.8 | async-start | bytes 2359296 | tf_op jit(solution)/shard_map/reduce_scatter | solution.py:92
  388.3 1.3 copy-start.1
  389.6 200.2 %all-reduce.8.cloned.1.call-start = ((), (), s32[]{:S(2)}) async-start(), calls=%async_computation.9 | async-start | bytes 131072 | tf_op jit(solution)/shard_map/psum | solution.py:59
  450.9 188.7 %all-gather.9.cloned.1.call-start = ((), (), s32[]{:S(2)}) async-start(), calls=%async_computation.10 | async-start | bytes 1179648 | tf_op jit(solution)/shard_map/all_gather | solution.py:82
  616.8 148.2 %reduce-scatter.9.cloned.1.call-start = ((), (), s32[]{:S(2)}) async-start(), calls=%async_computation.11 | async-start | bytes 4456448 | tf_op jit(solution)/shard_map/reduce_scatter | solution.py:86
  657.9 248.7 %all-reduce.10.cloned.1.call-start = ((), (), s32[]{:S(2)}) async-start(), calls=%async_computation.12 | async-start | bytes 131072 | tf_op jit(solution)/shard_map/psum | solution.py:59
  767.2 210.9 %all-gather.11.cloned.1.call-start = ((), (), s32[]{:S(2)}) async-start(), calls=%async_computation.13 | async-start | bytes 2228224 | tf_op jit(solution)/shard_map/all_gather | solution.py:88
  933.6 119.3 %reduce-scatter.11.cloned.1.call-start = ((), (), s32[]{:S(2)}) async-start(), calls=%async_computation.14 | async-start | bytes 2359296 | tf_op jit(solution)/shard_map/reduce_scatter | solution.py:92
  978.3 77.1 %copy-start.2 = (bf16[4096,128]{1,0:T(8,128)(2,1)S(1)}, bf16[4096,128]{1,0:T(8,128)(2,1)}, u32[]{:S(2)}) copy-start(bf16[4096,128]{1,0:T(8,128)(2,1)} %param.24) | copy-start | bytes 3145732
  992.5 1.3 copy-start
  993.8 200.2 %all-reduce.12.cloned.1.call-start = ((), (), s32[]{:S(2)}) async-start(), calls=%async_computation.15 | async-start | bytes 131072 | tf_op jit(solution)/shard_map/psum | solution.py:59
  1055.1 324.0 %all-reduce.14.cloned.1.call-start = ((), (), s32[]{:S(2)}) async-start(), calls=%async_computation.16 | async-start | bytes 4194304 | tf_op jit(solution)/shard_map/psum | solution.py:109
Sparse Core Ops, SparseCore 0:
  9.7 25.7 all-gather.4
  53.9 106.9 reduce-scatter.4
  166.1 136.2 all-reduce.5
  329.5 44.4 all-gather.6
  389.7 58.8 reduce-scatter.6
  453.8 135.9 all-reduce.7
  616.9 22.6 all-gather.8
  658.0 106.9 reduce-scatter.8
  770.3 136.2 all-reduce.9
  933.7 44.4 all-gather.10
  994.0 58.8 reduce-scatter.10
  1058.0 135.9 all-reduce.11
  1228.2 150.8 all-reduce.13
where the time goes:
time: 1400 us; the launch traced here: 1390 us
  waiting for transfers between devices  1110 us (79%)
  other arithmetic  107 us (8%)
  blocking collectives  66.9 us (5%)
  matrix products  49.2 us (4%)
  local copies, waits for them, and re-layouts  22.5 us (2%)
  loops' own time  18.5 us (1%)
  between operations  14.4 us (1%)
    psum x4, waiting for transfers between devices, orthonormal(): gram_matrix = lax.psum(local_gram(product), ('row', 'col')) / total_rows  555 us
    reduce_scatter x2, waiting for transfers between devices, shards(): lax.psum_scatter(partial_sum, 'row', scatter_dimension=0, tiled=True)  214 us
    reduce_scatter x2, waiting for transfers between devices, shards(): lax.psum_scatter(partial_sum, 'col', scatter_dimension=0, tiled=True)  118 us
    all_gather x2, waiting for transfers between devices, shards(): gathered = lax.all_gather(factor, 'row', axis=0, tiled=True)  89 us
    psum x1, waiting for transfers between devices, shards(): all_sums, all_totals = lax.psum((sums, totals), ('row', 'col'))  83.4 us
    psum x1, blocking collectives, shards(): all_sums, all_totals = lax.psum((sums, totals), ('row', 'col'))  66.9 us
    another operation x12, other arithmetic, finish(): lower_factor = jnp.linalg.cholesky(gram_matrix)  49.6 us
    all_gather x2, waiting for transfers between devices, shards(): gathered = lax.all_gather(panel, 'col', axis=0, tiled=True)  48.7 us
  transfers between devices with their start and end apart: 13, of which 13 were waited for; matrix products, arithmetic and copies ran while one was open for 0% of the time, Pallas kernels for 0%

commit v1 on v0

v1 whole, which is shorter than its diff:
```python
import jax
import jax.numpy as jnp
from jax import lax
from jax.experimental import pallas as pl
from jax.experimental.pallas import tpu as pltpu
from jax.sharding import PartitionSpec as P

ROUNDS = 2
SHARPNESS = 48.0
EPS = 1e-06

SIDE = 4
BF = jnp.bfloat16
F32 = jnp.float32
HIGHEST = lax.Precision.HIGHEST


def dot(a, b, contract, precision=None):
    return lax.dot_general(
        a, b, ((contract[:1], contract[1:]), ((), ())), precision=precision,
        preferred_element_type=F32,
    )


def shift_row(value, dx, dz):
    pairs = [
        (x * SIDE + z, (x + dx) % SIDE * SIDE + (z + dz) % SIDE)
        for x in range(SIDE)
        for z in range(SIDE)
    ]
    return lax.ppermute(value, "row", pairs)


def shift_col(value, dy, dc):
    pairs = [
        (y * 2 + c, (y + dy) % SIDE * 2 + (c + dc) % 2) for y in range(SIDE) for c in range(2)
    ]
    return lax.ppermute(value, "col", pairs)


def sum_row(value):
    value = value + shift_row(value, 1, 0) + shift_row(value, 2, 0) + shift_row(value, 3, 0)
    return value + shift_row(value, 0, 1) + shift_row(value, 0, 2) + shift_row(value, 0, 3)


def sum_col(value):
    value = value + shift_col(value, 1, 0) + shift_col(value, 2, 0) + shift_col(value, 3, 0)
    return value + shift_col(value, 0, 1)


def whole(shape):
    return pl.BlockSpec(shape, lambda *_: (0,) * len(shape))


def small_call(body, name, out_shapes, *args):
    return pl.pallas_call(body, out_shape=out_shapes, name=name)(*args)


def down_body(meta, weights, mine, theirs, tile, out, acc, rows):
    step = pl.program_id(0)
    half = mine.shape[1]

    @pl.when(step == 0)
    def _():
        acc[...] = jnp.zeros_like(acc)

    @pl.when(step < meta[12])
    def _():
        place = (meta[13] + SIDE - meta[step]) % SIDE
        core = meta[14]
        rows[pl.ds(pl.multiple_of(core * half, half), half), :] = mine[place]
        rows[pl.ds(pl.multiple_of((1 - core) * half, half), half), :] = theirs[place]
        product = dot(rows[...], tile[0], (0, 0))
        target = meta[6 + step]
        acc[target] = acc[target] + weights[step] * product

    @pl.when(step == pl.num_programs(0) - 1)
    def _():
        for block in range(acc.shape[0]):
            out[2 * block] = acc[block, :, :half].astype(BF)
            out[2 * block + 1] = acc[block, :, half:].astype(BF)


def up_body(meta, weights, gathered, tile, keep, send, acc):
    step = pl.program_id(0)
    half = gathered.shape[2]

    @pl.when(step == 0)
    def _():
        acc[...] = jnp.zeros_like(acc)

    @pl.when(step < meta[12])
    def _():
        source = meta[6 + step]
        product = dot(tile[0, :, :half], gathered[2 * source], (1, 1))
        product += dot(tile[0, :, half:], gathered[2 * source + 1], (1, 1))
        target = meta[step]
        acc[target] = acc[target] + weights[step] * product

    @pl.when(step == pl.num_programs(0) - 1)
    def _():
        core = meta[14]
        for block in range(acc.shape[0]):
            keep[block] = acc[block, pl.ds(pl.multiple_of(core * half, half), half), :]
            send[block] = acc[block, pl.ds(pl.multiple_of((1 - core) * half, half), half), :]


def tile_call(body, name, meta, weights, panels, tiles, outs, scratch):
    slots, block, _ = tiles.shape
    rank = 128
    grid_spec = pltpu.PrefetchScalarGridSpec(
        num_scalar_prefetch=1,
        grid=(slots,),
        in_specs=[pl.BlockSpec(memory_space=pltpu.SMEM)]
        + [pl.BlockSpec(p.shape, lambda i, meta, n=p.ndim: (0,) * n) for p in panels]
        + [pl.BlockSpec((1, block, block), lambda i, meta: (jnp.minimum(i, meta[12] - 1), 0, 0))],
        out_specs=[pl.BlockSpec(o.shape, lambda i, meta, n=len(o.shape): (0,) * n) for o in outs],
        scratch_shapes=scratch,
    )
    return pl.pallas_call(
        body,
        grid_spec=grid_spec,
        out_shape=outs,
        name=name,
        cost_estimate=pl.CostEstimate(
            flops=2 * slots * block * block * rank,
            transcendentals=0,
            bytes_accessed=slots * block * block * 2 + 4 * 1024 * 1024,
        ),
    )(meta, weights, *panels, tiles)


def reduce_first_body(parts, out):
    out[...] = jnp.sum(parts[...].astype(F32), axis=0).astype(BF)


def reduce_down_body(parts, inverse, out):
    total = jnp.sum(parts[...].astype(F32), axis=0)
    out[...] = dot(inverse[...], total, (1, 0), HIGHEST).astype(BF)


def fold_body(where, keep, got, own, one, two, three):
    at = where[0]
    own[...] = keep[at] + got[at]
    for distance, out in ((1, one), (2, two), (3, three)):
        to = (at + distance) % SIDE
        out[...] = (keep[to] + got[to]).astype(BF)


def reduce_up_body(own, one, two, three, inverse, out):
    total = own[...] + one[...].astype(F32) + two[...].astype(F32) + three[...].astype(F32)
    out[...] = dot(total, inverse[...], (1, 1), HIGHEST).astype(BF)


def reduce_last_body(own, one, two, three, inverse, out, gram):
    total = own[...] + one[...].astype(F32) + two[...].astype(F32) + three[...].astype(F32)
    total = dot(total, inverse[...], (1, 1), HIGHEST)
    out[...] = total
    gram[...] = dot(total, total, (0, 0), HIGHEST)


def gram_wide_body(parts, out):
    total = jnp.zeros(out.shape, F32)
    for part in range(parts.shape[0]):
        total += dot(parts[part], parts[part], (1, 1))
    out[...] = total


def gram_tall_body(mine, theirs, out):
    total = jnp.zeros(out.shape, F32)
    for part in range(mine.shape[0]):
        total += dot(mine[part], mine[part], (0, 0))
        total += dot(theirs[part], theirs[part], (0, 0))
    out[...] = total


def inverse_factor(gram, total_rows):
    lower = jnp.linalg.cholesky(gram / total_rows)
    identity = jnp.eye(gram.shape[0], dtype=F32)
    return lax.linalg.triangular_solve(lower, identity, left_side=True, lower=True)


def cluster_body(product, inverse, centroids, panel, sums, totals, norms):
    step = pl.program_id(0)

    @pl.when(step == 0)
    def _():
        values = centroids[...].astype(F32)
        norms[...] = jnp.sum(values * values, axis=1, keepdims=True)
        sums[...] = jnp.zeros_like(sums)
        totals[...] = jnp.zeros_like(totals)

    rows = dot(product[...], inverse[...], (1, 1), HIGHEST).astype(BF)
    panel[...] = rows
    values = rows.astype(F32)
    length = jnp.sqrt(jnp.sum(values * values, axis=1, keepdims=True) + EPS)
    points = (values / length).astype(BF)
    affinity = dot(centroids[...], points, (1, 1))
    scores = SHARPNESS * (2.0 * affinity - norms[...])
    shifted = jnp.exp(scores - jnp.max(scores, axis=0, keepdims=True))
    resp = (shifted / jnp.sum(shifted, axis=0, keepdims=True)).astype(BF)
    sums[...] += dot(resp, points, (1, 0))
    totals[...] += dot(jnp.ones((8, resp.shape[1]), BF), resp, (1, 1))


def cluster(product, inverse, centroids, chunk):
    rows, rank = product.shape
    count = centroids.shape[0]
    return pl.pallas_call(
        cluster_body,
        grid=(rows // chunk,),
        in_specs=[
            pl.BlockSpec((chunk, rank), lambda i: (i, 0)),
            whole(inverse.shape),
            whole(centroids.shape),
        ],
        out_specs=[
            pl.BlockSpec((chunk, rank), lambda i: (i, 0)),
            whole((count, rank)),
            whole((8, count)),
        ],
        out_shape=[
            jax.ShapeDtypeStruct((rows, rank), BF),
            jax.ShapeDtypeStruct((count, rank), F32),
            jax.ShapeDtypeStruct((8, count), F32),
        ],
        scratch_shapes=[pltpu.VMEM((count, 1), F32)],
        name="cluster",
    )(product, inverse, centroids)


def pack_body(sums, totals, out):
    share = sums.shape[0] // out.shape[0]
    lanes = sums.shape[1]
    for piece in range(out.shape[0]):
        out[piece, :share, :] = sums[piece * share : (piece + 1) * share, :].astype(BF)
        ends = [
            totals[0:1, piece * share + k * lanes : piece * share + (k + 1) * lanes]
            for k in range(share // lanes)
        ]
        value = jnp.concatenate(ends, axis=0)
        high = value.astype(BF).astype(F32)
        tail = jnp.concatenate(
            [high, value - high, jnp.zeros((16 - 2 * len(ends), lanes), F32)], axis=0
        )
        out[piece, share:, :] = tail.astype(BF)


def gathered_sum_body(parts, out):
    out[...] = jnp.sum(parts[...].astype(F32), axis=0)


def centers_body(where, first, second, third, fourth, centroids, out):
    at = where[0]
    parts = (first, second, third, fourth)
    stack = [part[...] for part in parts]
    total = jnp.zeros_like(stack[0])
    for y in range(SIDE):
        place = (at + SIDE - y) % SIDE
        pick = stack[0]
        for k in range(1, SIDE):
            pick = jnp.where(place == k, stack[k], pick)
        total = total + pick
    share = out.shape[0]
    lanes = out.shape[1]
    mass = total[share : share + share // lanes] + total[share + share // lanes : share + 2 * (share // lanes)]
    for k in range(share // lanes):
        column = jnp.transpose(jnp.broadcast_to(mass[k : k + 1], (lanes, lanes)))
        block = slice(k * lanes, (k + 1) * lanes)
        out[block, :] = (
            (total[block] + centroids[block].astype(F32)) / (column + 1.0)
        ).astype(BF)


def shards(tiles, tile_list, tile_count, scale_index, scales, panel_start, centroids):
    block_size = tiles.shape[1]
    piece, rank = panel_start.shape
    rows_axis = lax.axis_size("row")
    cols_axis = lax.axis_size("col")
    total_rows = piece * rows_axis * cols_axis
    row_at = lax.axis_index("row")
    col_at = lax.axis_index("col")
    row_blocks = piece * cols_axis // block_size
    col_blocks = piece * rows_axis // block_size
    meta = jnp.concatenate(
        [
            tile_list[:, 0] - row_at * row_blocks,
            tile_list[:, 1] - col_at * col_blocks,
            tile_count,
            jnp.stack([col_at // 2, col_at % 2]).astype(jnp.int32),
        ]
    )
    where = (col_at // 2).astype(jnp.int32)[None]
    table_ids = jnp.arange(scales.shape[0], dtype=jnp.int32)
    weights = jnp.sum(
        jnp.where(scale_index[:, None] == table_ids[None, :], scales[None, :], 0.0), axis=1
    )
    square = jax.ShapeDtypeStruct((rank, rank), F32)
    tall = jax.ShapeDtypeStruct((piece, rank), BF)
    tall_f32 = jax.ShapeDtypeStruct((piece, rank), F32)
    wide = jax.ShapeDtypeStruct((rank, piece), BF)
    smem = pl.BlockSpec(memory_space=pltpu.SMEM)
    vmem = pl.BlockSpec(memory_space=pltpu.VMEM)

    panel = panel_start
    inverse = None
    for round_index in range(ROUNDS):
        mine = jnp.stack([panel] + [shift_col(panel, d, 0) for d in (1, 2, 3)])
        theirs = shift_col(mine, 0, 1)
        if round_index > 0:
            gram = sum_row(small_call(gram_tall_body, "gram_tall", square, mine, theirs))
            inverse = inverse_factor(gram, total_rows)
        (partial,) = tile_call(
            down_body, "down", meta, weights, [mine, theirs], tiles,
            [jax.ShapeDtypeStruct((rows_axis, rank, piece), BF)],
            [pltpu.VMEM((col_blocks, rank, block_size), F32), pltpu.VMEM((block_size, rank), BF)],
        )
        parts = lax.all_to_all(partial, "row", 0, 0, tiled=True)
        if inverse is None:
            factor = small_call(reduce_first_body, "reduce_first", wide, parts)
        else:
            factor = small_call(reduce_down_body, "reduce_down", wide, parts, inverse)
        copies = jnp.broadcast_to(factor[None], (rows_axis,) + factor.shape)
        gathered = lax.all_to_all(copies, "row", 0, 0, tiled=True)
        gram = sum_col(small_call(gram_wide_body, "gram_wide", square, gathered))
        inverse = inverse_factor(gram, total_rows)
        keep, send = tile_call(
            up_body, "up", meta, weights, [gathered], tiles,
            [jax.ShapeDtypeStruct((SIDE, piece, rank), F32)] * 2,
            [pltpu.VMEM((row_blocks, block_size, rank), F32)],
        )
        got = shift_col(send, 0, 1)
        own, one, two, three = pl.pallas_call(
            fold_body,
            in_specs=[smem, vmem, vmem],
            out_shape=[tall_f32, tall, tall, tall],
            name="fold",
        )(where, keep, got)
        one, two, three = shift_col(one, 1, 0), shift_col(two, 2, 0), shift_col(three, 3, 0)
        if round_index + 1 < ROUNDS:
            panel = small_call(reduce_up_body, "reduce_up", tall, own, one, two, three, inverse)
        else:
            product, gram = small_call(
                reduce_last_body, "reduce_last", [tall_f32, square], own, one, two, three, inverse
            )
    inverse = inverse_factor(sum_col(sum_row(gram)), total_rows)

    panel, sums, totals = cluster(product, inverse, centroids, 256)
    count = centroids.shape[0]
    share = count // rows_axis
    packed = small_call(
        pack_body, "pack", jax.ShapeDtypeStruct((rows_axis, share + 16, rank), BF), sums, totals
    )
    parts = lax.all_to_all(packed, "row", 0, 0, tiled=True)
    mass = small_call(
        gathered_sum_body, "mass", jax.ShapeDtypeStruct((share + 16, rank), F32), parts
    )
    mass = mass + shift_col(mass, 0, 1)
    owned = lax.dynamic_slice_in_dim(centroids, row_at * share, share, 0)
    centers = pl.pallas_call(
        centers_body,
        in_specs=[smem] + [vmem] * 5,
        out_shape=jax.ShapeDtypeStruct((share, rank), BF),
        name="centers",
    )(where, mass, shift_col(mass, 1, 0), shift_col(mass, 2, 0), shift_col(mass, 3, 0), owned)
    copies = jnp.broadcast_to(centers[None], (rows_axis,) + centers.shape)
    centers = lax.all_to_all(copies, "row", 0, 0, tiled=True)
    return (panel, centers.reshape(count, rank).astype(F32))


def solution(mesh):
    return jax.shard_map(
        shards,
        mesh=mesh,
        in_specs=(
            P(("row", "col"), None, None),
            P(("row", "col"), None),
            P(("row", "col")),
            P(("row", "col")),
            P(),
            P(("row", "col"), None),
            P(),
        ),
        out_specs=(P(("row", "col"), None), P()),
        check_vma=False,
    )
```

time: 1400 us -> 479 us (0.34)
  waiting for transfers between devices: 1110 us -> 67.4 us
  blocking collectives: 66.9 us -> 142 us
  Pallas kernels: 0 us -> 71.6 us
  starting transfers between devices: 1.44 us -> 73 us
  matrix products: 49.2 us -> 3.65 us
  loops' own time: 18.5 us -> 0 us
    psum x5 -> x0, waiting for transfers between devices: 638 us -> none  [the longest x4 555 us: orthonormal(): gram_matrix = lax.psum(local_gram(product), ('row', 'col')) / total_rows]
    reduce_scatter x4 -> x0, waiting for transfers between devices: 332 us -> none  [the longest x2 214 us: shards(): lax.psum_scatter(partial_sum, 'row', scatter_dimension=0, tiled=True)]
    all_to_all x0 -> x5, blocking collectives: none -> 142 us  [the longest x2 59.3 us: shards(): gathered = lax.all_to_all(copies, 'row', 0, 0, tiled=True)]
    all_gather x4 -> x0, waiting for transfers between devices: 138 us -> none  [the longest x2 89 us: shards(): gathered = lax.all_gather(factor, 'row', axis=0, tiled=True)]
    pallas_call x0 -> x17, Pallas kernels: none -> 71.6 us  [the longest x4 29.7 us: tile_call(): pl.pallas_call(body, grid_spec=grid_spec, out_shape=outs, name=name, cost...]
    ppermute x0 -> x44, waiting for transfers between devices: none -> 67.4 us  [the longest x32 40.3 us: shift_col(): return lax.ppermute(value, 'col', pairs)]
    psum x1 -> x0, blocking collectives: 66.9 us -> none  [shards(): all_sums, all_totals = lax.psum((sums, totals), ('row', 'col'))]
    ppermute x0 -> x44, starting transfers between devices: none -> 65.8 us  [the longest x32 44.7 us: shift_col(): return lax.ppermute(value, 'col', pairs)]
  transfers between devices with their start and end apart: 13 -> 45, of which waited for: 13 -> 26; matrix products, arithmetic and copies ran while one was open for 0% -> 16% of each run, Pallas kernels for 0% -> 4%
where the time goes in v1:
time: 479 us; the launch traced here: 474 us
  blocking collectives  142 us (30%)
  other arithmetic  98.2 us (21%)
  starting transfers between devices  73 us (15%)
  Pallas kernels  71.6 us (15%)
  waiting for transfers between devices  67.4 us (14%)
  local copies, waits for them, and re-layouts  16.4 us (3%)
    all_to_all x2, blocking collectives, shards(): gathered = lax.all_to_all(copies, 'row', 0, 0, tiled=True)  59.3 us
    another operation x12, other arithmetic, inverse_factor(): lower = jnp.linalg.cholesky(gram / total_rows)  49.6 us
    ppermute x32, starting transfers between devices, shift_col(): return lax.ppermute(value, 'col', pairs)  44.7 us
    another operation x8, other arithmetic, inverse_factor(): lax.linalg.triangular_solve(lower, identity, left_side=True, lower=True)  41.9 us
    ppermute x32, waiting for transfers between devices, shift_col(): return lax.ppermute(value, 'col', pairs)  40.3 us
    all_to_all x1, blocking collectives, shards(): parts = lax.all_to_all(partial, 'row', 0, 0, tiled=True)  36.8 us
    pallas_call x4, Pallas kernels, tile_call(): pl.pallas_call(body, grid_spec=grid_spec, out_shape=outs, name=name, cost...  29.7 us
    ppermute x12, waiting for transfers between devices, shift_row(): return lax.ppermute(value, 'row', pairs)  27 us
  transfers between devices with their start and end apart: 45, of which 26 were waited for; matrix products, arithmetic and copies ran while one was open for 16% of the time, Pallas kernels for 4%

profile of v1, /device:TPU:0, one launch (start us, length us, event | category | flops | bytes accessed | tf_op | source)
XLA Modules:
  0.0 474.0 jit_solution(7952470957915858761)
XLA Ops:
  2.4 2.9 collective-permute-start.1
  7.5 4.0 collective-permute-done.1
  16.9 7.1 %down.2 = bf16[16,128,512]{2,1,0:T(8,128)(2,1)} custom-call(s32[15]{0:T(128)} %concatenate.3.meta, f32[6]{0:T(128)} %select_reduce_fusion.4.weights, bf16[4,512,128]{2,1,0:T(8,128)(2,1)} %copy-done.2, bf16[4,512,128]{2,1,0:T(8,128)(2,1)} %copy-done.7, bf16[6,1024,1024]{2,1,0:T(8,128)(2,1)} %tile.7), custom_call_target="tpu_custom_call" | custom-call | flops 1610612736 | bytes 16777216 | tf_op jit(solution)/shard_map/down/pallas_call | solution.py:120
  24.0 36.8 %all_to_all.30.parts = bf16[16,128,512]{2,1,0:T(8,128)(2,1)} all-to-all(bf16[16,128,512]{2,1,0:T(8,128)(2,1)} %down.2), channel_id=1, replica_groups=mesh['row'=16,'col'=8] {'row'}, dimensions={0} | all-to-all | bytes 4194304 | tf_op jit(solution)/shard_map/all_to_all | solution.py:318
  60.8 2.5 reduce_first.1
  64.4 29.7 %all_to_all.31.gathered.parts = bf16[16,128,512]{2,1,0:T(8,128)(2,1)} all-to-all(bf16[16,128,512]{2,1,0:T(8,128)(2,1)S(1)} %broadcast_in_dim.24), channel_id=1, replica_groups=mesh['row'=16,'col'=8] {'row'}, dimensions={0} | all-to-all | bytes 4194304 | tf_op jit(solution)/shard_map/all_to_all | solution.py:324
  94.2 2.9 gram_wide.2
  98.0 3.6 collective-permute-start.10
  103.0 2.6 collective-permute-start.9
  105.6 7.7 %up.2 = (f32[4,512,128]{2,1,0:T(8,128)}, f32[4,512,128]{2,1,0:T(8,128)}) custom-call(s32[15]{0:T(128)} %concatenate.3.meta, f32[6]{0:T(128)} %select_reduce_fusion.4.weights, bf16[16,128,512]{2,1,0:T(8,128)(2,1)} %all_to_all.31.gathered.parts, bf16[6,1024,1024]{2,1,0:T(8,128)(2,1)} %tile.7), custom_call_target="tpu_custom_call" | custom-call | flops 1610612736 | bytes 16777216 | tf_op jit(solution)/shard_map/up/pallas_call | solution.py:120
  116.4 11.7 %cholesky.74 = f32[128,128]{1,0:T(8,128)S(1)} custom-call(f32[128,128]{1,0:T(8,128)S(1)} %fusion.19), custom_call_target="Cholesky" | custom-call | tf_op jit(solution)/shard_map/jit(cholesky)/cholesky | solution.py:178
  129.4 9.8 %custom-call.8 = f32[1,128,128]{1,2,0:T(8,128)S(1)} custom-call(f32[1,128,128]{2,1,0:T(8,128)S(1)} %fusion.8), custom_call_target="InvertDiagBlocksLowerTriangular" | custom-call | tf_op jit(solution)/shard_map/triangular_solve/custom-call.0 | solution.py:180
  140.2 2.5 fold.2
  142.9 4.2 collective-permute-start.6
  149.7 3.9 collective-permute-done.6.two
  156.4 3.5 collective-permute-start.13
  160.0 3.1 collective-permute-done.12
  163.0 3.4 collective-permute-done.13
  170.2 7.1 %down.3 = bf16[16,128,512]{2,1,0:T(8,128)(2,1)} custom-call(s32[15]{0:T(128)} %concatenate.3.meta, f32[6]{0:T(128)} %select_reduce_fusion.4.weights, bf16[4,512,128]{2,1,0:T(8,128)(2,1)} %copy-done.1, bf16[4,512,128]{2,1,0:T(8,128)(2,1)} %copy-done.3, bf16[6,1024,1024]{2,1,0:T(8,128)(2,1)} %tile.7), custom_call_target="tpu_custom_call" | custom-call | flops 1610612736 | bytes 16777216 | tf_op jit(solution)/shard_map/down/pallas_call | solution.py:120
  177.4 7.2 %all-to-all-start.2 = ((bf16[16,128,512]{2,1,0:T(8,128)(2,1)}), bf16[16,128,512]{2,1,0:T(8,128)(2,1)S(1)}, u32[]{:S(2)}, u32[]{:S(2)}) async-start(bf16[16,128,512]{2,1,0:T(8,128)(2,1)} %down.3), calls=%async_computation.2 | async-start | bytes 4194304 | tf_op jit(solution)/shard_map/all_to_all | solution.py:318
  189.8 2.7 collective-permute-start.17
  194.0 17.8 %collective-permute-done.16 = f32[128,128]{0,1:T(8,128)S(1)} collective-permute-done((f32[128,128]{0,1:T(8,128)S(1)}, f32[128,128]{0,1:T(8,128)S(1)}, u32[]{:S(2)}, u32[]{:S(2)}) %collective-permute-start.16) | collective-permute-done | bytes 65568 | tf_op jit(solution)/shard_map/ppermute | solution.py:31
  214.5 2.6 collective-permute-start.20
  221.5 11.7 %cholesky.85 = f32[128,128]{1,0:T(8,128)S(1)} custom-call(f32[128,128]{1,0:T(8,128)S(1)} %fusion.17), custom_call_target="Cholesky" | custom-call | tf_op jit(solution)/shard_map/jit(cholesky)/cholesky | solution.py:178
  234.6 9.8 %custom-call.9 = f32[1,128,128]{1,2,0:T(8,128)S(1)} custom-call(f32[1,128,128]{2,1,0:T(8,128)S(1)} %fusion.9), custom_call_target="InvertDiagBlocksLowerTriangular" | custom-call | tf_op jit(solution)/shard_map/triangular_solve/custom-call.0 | solution.py:180
  246.6 2.9 reduce_down.1
  250.7 29.5 %all_to_all.32.gathered.parts = bf16[16,128,512]{2,1,0:T(8,128)(2,1)} all-to-all(bf16[16,128,512]{2,1,0:T(8,128)(2,1)S(1)} %broadcast_in_dim.25), channel_id=1, replica_groups=mesh['row'=16,'col'=8] {'row'}, dimensions={0} | all-to-all | bytes 4194304 | tf_op jit(solution)/shard_map/all_to_all | solution.py:324
  280.2 2.9 gram_wide.3
  285.5 5.0 %collective-permute-start.27 = (f32[128,128]{0,1:T(8,128)S(1)}, f32[128,128]{0,1:T(8,128)S(1)}, u32[]{:S(2)}, u32[]{:S(2)}) collective-permute-start(f32[128,128]{0,1:T(8,128)S(1)} %copy.40), channel_id=1, source_target_pairs={{0,4},{1,5},{2,6},{3,7},{4,0},{5,1},{6,2},{7,3},{8,12},{9,13},{10,... | collective-permute-start | bytes 196616 | tf_op jit(solution)/shard_map/ppermute | solution.py:38
  290.5 2.5 collective-permute-start.28
  293.0 7.7 %up.3 = (f32[4,512,128]{2,1,0:T(8,128)}, f32[4,512,128]{2,1,0:T(8,128)}) custom-call(s32[15]{0:T(128)} %concatenate.3.meta, f32[6]{0:T(128)} %select_reduce_fusion.4.weights, bf16[16,128,512]{2,1,0:T(8,128)(2,1)} %all_to_all.32.gathered.parts, bf16[6,1024,1024]{2,1,0:T(8,128)(2,1)} %tile.7), custom_call_target="tpu_custom_call" | custom-call | flops 1610612736 | bytes 16777216 | tf_op jit(solution)/shard_map/up/pallas_call | solution.py:120
  303.8 11.7 %cholesky.96 = f32[128,128]{1,0:T(8,128)S(1)} custom-call(f32[128,128]{1,0:T(8,128)S(1)} %fusion.15), custom_call_target="Cholesky" | custom-call | tf_op jit(solution)/shard_map/jit(cholesky)/cholesky | solution.py:178
  316.9 9.8 %custom-call.10 = f32[1,128,128]{1,2,0:T(8,128)S(1)} custom-call(f32[1,128,128]{2,1,0:T(8,128)S(1)} %fusion.10), custom_call_target="InvertDiagBlocksLowerTriangular" | custom-call | tf_op jit(solution)/shard_map/triangular_solve/custom-call.0 | solution.py:180
  327.7 2.5 fold.3
  330.2 2.3 collective-permute-start.24
  334.3 5.6 %collective-permute-done.23.one = bf16[512,128]{1,0:T(8,128)(2,1)S(1)} collective-permute-done((bf16[512,128]{1,0:T(8,128)(2,1)}, bf16[512,128]{1,0:T(8,128)(2,1)S(1)}, u32[]{:S(2)}, u32[]{:S(2)}) %collective-permute-start.23) | collective-permute-done | bytes 131104 | tf_op jit(solution)/shard_map/ppermute | solution.py:38
  341.2 2.8 reduce_last.1
  348.6 2.7 collective-permute-done.30
  355.1 2.5 collective-permute-start.35
  360.4 3.1 collective-permute-start.37
  369.4 11.7 %cholesky.107 = f32[128,128]{1,0:T(8,128)S(1)} custom-call(f32[128,128]{1,0:T(8,128)S(1)} %fusion.13), custom_call_target="Cholesky" | custom-call | tf_op jit(solution)/shard_map/jit(cholesky)/cholesky | solution.py:178
  382.4 9.8 %custom-call.11 = f32[1,128,128]{1,2,0:T(8,128)S(1)} custom-call(f32[1,128,128]{2,1,0:T(8,128)S(1)} %fusion.11), custom_call_target="InvertDiagBlocksLowerTriangular" | custom-call | tf_op jit(solution)/shard_map/triangular_solve/custom-call.0 | solution.py:180
  393.2 11.7 %cluster.1 = (bf16[512,128]{1,0:T(8,128)(2,1)}, f32[4096,128]{1,0:T(8,128)}, f32[8,4096]{1,0:T(8,128)}) custom-call(f32[512,128]{1,0:T(8,128)} %get-tuple-element.33.product, f32[128,128]{1,0:T(8,128)} %fusion.inverse, bf16[4096,128]{1,0:T(8,128)(2,1)} %centroids.1), custom_call_target="tpu_custom_call" | custom-call | tf_op jit(solution)/shard_map/cluster/pallas_call | solution.py:209
  404.9 2.7 pack.1
  407.6 26.2 %all_to_all.33.parts = bf16[16,272,128]{2,1,0:T(8,128)(2,1)} all-to-all(bf16[16,272,128]{2,1,0:T(8,128)(2,1)} %pack.1), channel_id=1, replica_groups=mesh['row'=16,'col'=8] {'row'}, dimensions={0} | all-to-all | bytes 2228224 | tf_op jit(solution)/shard_map/all_to_all | solution.py:354
  438.8 2.8 collective-permute-start.42
  444.1 4.3 collective-permute-done.41.second
  452.7 19.6 %all_to_all.34 = bf16[16,256,128]{2,1,0:T(8,128)(2,1)S(1)} all-to-all(bf16[16,256,128]{2,1,0:T(8,128)(2,1)S(1)} %broadcast_in_dim.42), channel_id=1, replica_groups=mesh['row'=16,'col'=8] {'row'}, dimensions={0} | all-to-all | bytes 2097152 | tf_op jit(solution)/shard_map/all_to_all | solution.py:367
  (155 shorter events, 88.5 us)
Async XLA Ops:
  0.6 6.9 %collective-permute-start = (bf16[512,128]{1,0:T(8,128)(2,1)}, bf16[512,128]{1,0:T(8,128)(2,1)S(1)}, u32[]{:S(2)}, u32[]{:S(2)}) collective-permute-start(bf16[512,128]{1,0:T(8,128)(2,1)} %param.15), channel_id=1, source_target_pairs={{0,2},{1,3},{2,4},{3,5},{4,6},{5,7},{6,0},{7,1},{8,10},{9,11},{10,... | collective-permute-start | bytes 393224 | tf_op jit(solution)/shard_map/ppermute | solution.py:38
  2.4 9.1 %collective-permute-start.1 = (bf16[512,128]{1,0:T(8,128)(2,1)}, bf16[512,128]{1,0:T(8,128)(2,1)S(1)}, u32[]{:S(2)}, u32[]{:S(2)}) collective-permute-start(bf16[512,128]{1,0:T(8,128)(2,1)} %param.15), channel_id=1, source_target_pairs={{0,4},{1,5},{2,6},{3,7},{4,0},{5,1},{6,2},{7,3},{8,12},{9,13},{10,... | collective-permute-start | bytes 393224 | tf_op jit(solution)/shard_map/ppermute | solution.py:38
  5.3 6.2 %collective-permute-start.2 = (bf16[512,128]{1,0:T(8,128)(2,1)}, bf16[512,128]{1,0:T(8,128)(2,1)S(1)}, u32[]{:S(2)}, u32[]{:S(2)}) collective-permute-start(bf16[512,128]{1,0:T(8,128)(2,1)} %param.15), channel_id=1, source_target_pairs={{0,6},{1,7},{2,0},{3,1},{4,2},{5,3},{6,4},{7,5},{8,14},{9,15},{10,... | collective-permute-start | bytes 393224 | tf_op jit(solution)/shard_map/ppermute | solution.py:38
  12.5 3.6 copy-start.2
  12.5 3.6 collective-permute-start.3
  98.0 15.3 %collective-permute-start.10 = (f32[128,128]{0,1:T(8,128)S(1)}, f32[128,128]{0,1:T(8,128)S(1)}, u32[]{:S(2)}, u32[]{:S(2)}) collective-permute-start(f32[128,128]{0,1:T(8,128)S(1)} %copy.30), channel_id=1, source_target_pairs={{0,6},{1,7},{2,0},{3,1},{4,2},{5,3},{6,4},{7,5},{8,14},{9,15},{10,... | collective-permute-start | bytes 196616 | tf_op jit(solution)/shard_map/ppermute | solution.py:38
  101.7 11.6 %collective-permute-start.8 = (f32[128,128]{0,1:T(8,128)S(1)}, f32[128,128]{0,1:T(8,128)S(1)}, u32[]{:S(2)}, u32[]{:S(2)}) collective-permute-start(f32[128,128]{0,1:T(8,128)S(1)} %copy.30), channel_id=1, source_target_pairs={{0,2},{1,3},{2,4},{3,5},{4,6},{5,7},{6,0},{7,1},{8,10},{9,11},{10,... | collective-permute-start | bytes 196616 | tf_op jit(solution)/shard_map/ppermute | solution.py:38
  103.0 10.3 %collective-permute-start.9 = (f32[128,128]{0,1:T(8,128)S(1)}, f32[128,128]{0,1:T(8,128)S(1)}, u32[]{:S(2)}, u32[]{:S(2)}) collective-permute-start(f32[128,128]{0,1:T(8,128)S(1)} %copy.30), channel_id=1, source_target_pairs={{0,4},{1,5},{2,6},{3,7},{4,0},{5,1},{6,2},{7,3},{8,12},{9,13},{10,... | collective-permute-start | bytes 196616 | tf_op jit(solution)/shard_map/ppermute | solution.py:38
  113.3 26.0 %collective-permute-start.4 = (f32[4,512,128]{2,1,0:T(8,128)}, f32[4,512,128]{2,1,0:T(8,128)S(1)}, u32[]{:S(2)}, u32[]{:S(2)}) collective-permute-start(f32[4,512,128]{2,1,0:T(8,128)} %get-tuple-element.22), channel_id=1, source_target_pairs={{0,1},{1,0},{2,3},{3,2},{4,5},{5,4},{6,7},{7,6},{8,9},{9,8},{10,11... | collective-permute-start | bytes 3145736 | tf_op jit(solution)/shard_map/ppermute | solution.py:38
  113.3 2.9 collective-permute-start.11
  142.7 7.0 %collective-permute-start.5 = (bf16[512,128]{1,0:T(8,128)(2,1)}, bf16[512,128]{1,0:T(8,128)(2,1)S(1)}, u32[]{:S(2)}, u32[]{:S(2)}) collective-permute-start(bf16[512,128]{1,0:T(8,128)(2,1)} %get-tuple-element.24), channel_id=1, source_target_pairs={{0,2},{1,3},{2,4},{3,5},{4,6},{5,7},{6,0},{7,1},{8,10},{9,11},{10,... | collective-permute-start | bytes 393224 | tf_op jit(solution)/shard_map/ppermute | solution.py:38
  142.9 10.7 %collective-permute-start.6 = (bf16[512,128]{1,0:T(8,128)(2,1)}, bf16[512,128]{1,0:T(8,128)(2,1)S(1)}, u32[]{:S(2)}, u32[]{:S(2)}) collective-permute-start(bf16[512,128]{1,0:T(8,128)(2,1)} %get-tuple-element.25), channel_id=1, source_target_pairs={{0,4},{1,5},{2,6},{3,7},{4,0},{5,1},{6,2},{7,3},{8,12},{9,13},{10,... | collective-permute-start | bytes 393224 | tf_op jit(solution)/shard_map/ppermute | solution.py:38
  147.1 6.5 %collective-permute-start.7 = (bf16[512,128]{1,0:T(8,128)(2,1)}, bf16[512,128]{1,0:T(8,128)(2,1)S(1)}, u32[]{:S(2)}, u32[]{:S(2)}) collective-permute-start(bf16[512,128]{1,0:T(8,128)(2,1)} %get-tuple-element.26), channel_id=1, source_target_pairs={{0,6},{1,7},{2,0},{3,1},{4,2},{5,3},{6,4},{7,5},{8,14},{9,15},{10,... | collective-permute-start | bytes 393224 | tf_op jit(solution)/shard_map/ppermute | solution.py:38
  149.7 4.0 copy-start.12
  156.4 6.6 %collective-permute-start.12 = (bf16[512,128]{1,0:T(8,128)(2,1)}, bf16[512,128]{1,0:T(8,128)(2,1)S(1)}, u32[]{:S(2)}, u32[]{:S(2)}) collective-permute-start(bf16[512,128]{1,0:T(8,128)(2,1)} %reduce_up.1), channel_id=1, source_target_pairs={{0,2},{1,3},{2,4},{3,5},{4,6},{5,7},{6,0},{7,1},{8,10},{9,11},{10,... | collective-permute-start | bytes 393224 | tf_op jit(solution)/shard_map/ppermute | solution.py:38
  156.4 9.9 %collective-permute-start.13 = (bf16[512,128]{1,0:T(8,128)(2,1)}, bf16[512,128]{1,0:T(8,128)(2,1)S(1)}, u32[]{:S(2)}, u32[]{:S(2)}) collective-permute-start(bf16[512,128]{1,0:T(8,128)(2,1)} %reduce_up.1), channel_id=1, source_target_pairs={{0,4},{1,5},{2,6},{3,7},{4,0},{5,1},{6,2},{7,3},{8,12},{9,13},{10,... | collective-permute-start | bytes 393224 | tf_op jit(solution)/shard_map/ppermute | solution.py:38
  160.0 6.5 %collective-permute-start.14 = (bf16[512,128]{1,0:T(8,128)(2,1)}, bf16[512,128]{1,0:T(8,128)(2,1)S(1)}, u32[]{:S(2)}, u32[]{:S(2)}) collective-permute-start(bf16[512,128]{1,0:T(8,128)(2,1)} %reduce_up.1), channel_id=1, source_target_pairs={{0,6},{1,7},{2,0},{3,1},{4,2},{5,3},{6,4},{7,5},{8,14},{9,15},{10,... | collective-permute-start | bytes 393224 | tf_op jit(solution)/shard_map/ppermute | solution.py:38
  167.4 2.0 collective-permute-start.15
  177.4 68.0 %all-to-all-start.2 = ((bf16[16,128,512]{2,1,0:T(8,128)(2,1)}), bf16[16,128,512]{2,1,0:T(8,128)(2,1)S(1)}, u32[]{:S(2)}, u32[]{:S(2)}) async-start(bf16[16,128,512]{2,1,0:T(8,128)(2,1)} %down.3), calls=%async_computation.2 | async-start | bytes 4194304 | tf_op jit(solution)/shard_map/all_to_all | solution.py:318
  187.8 23.9 %collective-permute-start.16 = (f32[128,128]{0,1:T(8,128)S(1)}, f32[128,128]{0,1:T(8,128)S(1)}, u32[]{:S(2)}, u32[]{:S(2)}) collective-permute-start(f32[128,128]{0,1:T(8,128)S(1)} %copy.35), channel_id=1, source_target_pairs={{0,32},{8,40},{16,48},{24,56},{32,64},{40,72},{48,80},{56,88},{64,... | collective-permute-start | bytes 196616 | tf_op jit(solution)/shard_map/ppermute | solution.py:31
  189.8 22.9 %collective-permute-start.17 = (f32[128,128]{0,1:T(8,128)S(1)}, f32[128,128]{0,1:T(8,128)S(1)}, u32[]{:S(2)}, u32[]{:S(2)}) collective-permute-start(f32[128,128]{0,1:T(8,128)S(1)} %copy.35), channel_id=1, source_target_pairs={{0,64},{8,72},{16,80},{24,88},{32,96},{40,104},{48,112},{56,120},{... | collective-permute-start | bytes 196616 | tf_op jit(solution)/shard_map/ppermute | solution.py:31
  192.5 20.2 %collective-permute-start.18 = (f32[128,128]{0,1:T(8,128)S(1)}, f32[128,128]{0,1:T(8,128)S(1)}, u32[]{:S(2)}, u32[]{:S(2)}) collective-permute-start(f32[128,128]{0,1:T(8,128)S(1)} %copy.35), channel_id=1, source_target_pairs={{0,96},{8,104},{16,112},{24,120},{32,0},{40,8},{48,16},{56,24},{64... | collective-permute-start | bytes 196616 | tf_op jit(solution)/shard_map/ppermute | solution.py:31
  212.8 5.8 %collective-permute-start.19 = (f32[128,128]{0,1:T(8,128)S(1)}, f32[128,128]{0,1:T(8,128)S(1)}, u32[]{:S(2)}, u32[]{:S(2)}) collective-permute-start(f32[128,128]{0,1:T(8,128)S(1)} %add_add_fusion.4), channel_id=1, source_target_pairs={{0,8},{8,16},{16,24},{24,0},{32,40},{40,48},{48,56},{56,32},{64,72... | collective-permute-start | bytes 196616 | tf_op jit(solution)/shard_map/ppermute | solution.py:31
  214.5 5.8 %collective-permute-start.20 = (f32[128,128]{0,1:T(8,128)S(1)}, f32[128,128]{0,1:T(8,128)S(1)}, u32[]{:S(2)}, u32[]{:S(2)}) collective-permute-start(f32[128,128]{0,1:T(8,128)S(1)} %add_add_fusion.4), channel_id=1, source_target_pairs={{0,16},{8,24},{16,0},{24,8},{32,48},{40,56},{48,32},{56,40},{64,80... | collective-permute-start | bytes 196616 | tf_op jit(solution)/shard_map/ppermute | solution.py:31
  217.1 4.3 collective-permute-start.21
  284.1 16.7 %collective-permute-start.26 = (f32[128,128]{0,1:T(8,128)S(1)}, f32[128,128]{0,1:T(8,128)S(1)}, u32[]{:S(2)}, u32[]{:S(2)}) collective-permute-start(f32[128,128]{0,1:T(8,128)S(1)} %copy.40), channel_id=1, source_target_pairs={{0,2},{1,3},{2,4},{3,5},{4,6},{5,7},{6,0},{7,1},{8,10},{9,11},{10,... | collective-permute-start | bytes 196616 | tf_op jit(solution)/shard_map/ppermute | solution.py:38
  285.5 15.3 %collective-permute-start.27 = (f32[128,128]{0,1:T(8,128)S(1)}, f32[128,128]{0,1:T(8,128)S(1)}, u32[]{:S(2)}, u32[]{:S(2)}) collective-permute-start(f32[128,128]{0,1:T(8,128)S(1)} %copy.40), channel_id=1, source_target_pairs={{0,4},{1,5},{2,6},{3,7},{4,0},{5,1},{6,2},{7,3},{8,12},{9,13},{10,... | collective-permute-start | bytes 196616 | tf_op jit(solution)/shard_map/ppermute | solution.py:38
  290.5 10.3 %collective-permute-start.28 = (f32[128,128]{0,1:T(8,128)S(1)}, f32[128,128]{0,1:T(8,128)S(1)}, u32[]{:S(2)}, u32[]{:S(2)}) collective-permute-start(f32[128,128]{0,1:T(8,128)S(1)} %copy.40), channel_id=1, source_target_pairs={{0,6},{1,7},{2,0},{3,1},{4,2},{5,3},{6,4},{7,5},{8,14},{9,15},{10,... | collective-permute-start | bytes 196616 | tf_op jit(solution)/shard_map/ppermute | solution.py:38
  300.7 26.0 %collective-permute-start.22 = (f32[4,512,128]{2,1,0:T(8,128)}, f32[4,512,128]{2,1,0:T(8,128)S(1)}, u32[]{:S(2)}, u32[]{:S(2)}) collective-permute-start(f32[4,512,128]{2,1,0:T(8,128)} %get-tuple-element.28), channel_id=1, source_target_pairs={{0,1},{1,0},{2,3},{3,2},{4,5},{5,4},{6,7},{7,6},{8,9},{9,8},{10,11... | collective-permute-start | bytes 3145736 | tf_op jit(solution)/shard_map/ppermute | solution.py:38
  300.8 2.9 collective-permute-start.29
  330.2 9.8 %collective-permute-start.23 = (bf16[512,128]{1,0:T(8,128)(2,1)}, bf16[512,128]{1,0:T(8,128)(2,1)S(1)}, u32[]{:S(2)}, u32[]{:S(2)}) collective-permute-start(bf16[512,128]{1,0:T(8,128)(2,1)} %get-tuple-element.30), channel_id=1, source_target_pairs={{0,2},{1,3},{2,4},{3,5},{4,6},{5,7},{6,0},{7,1},{8,10},{9,11},{10,... | collective-permute-start | bytes 393224 | tf_op jit(solution)/shard_map/ppermute | solution.py:38
  330.2 9.8 %collective-permute-start.24 = (bf16[512,128]{1,0:T(8,128)(2,1)}, bf16[512,128]{1,0:T(8,128)(2,1)S(1)}, u32[]{:S(2)}, u32[]{:S(2)}) collective-permute-start(bf16[512,128]{1,0:T(8,128)(2,1)} %get-tuple-element.31), channel_id=1, source_target_pairs={{0,4},{1,5},{2,6},{3,7},{4,0},{5,1},{6,2},{7,3},{8,12},{9,13},{10,... | collective-permute-start | bytes 393224 | tf_op jit(solution)/shard_map/ppermute | solution.py:38
  332.5 8.1 %collective-permute-start.25 = (bf16[512,128]{1,0:T(8,128)(2,1)}, bf16[512,128]{1,0:T(8,128)(2,1)S(1)}, u32[]{:S(2)}, u32[]{:S(2)}) collective-permute-start(bf16[512,128]{1,0:T(8,128)(2,1)} %get-tuple-element.32), channel_id=1, source_target_pairs={{0,6},{1,7},{2,0},{3,1},{4,2},{5,3},{6,4},{7,5},{8,14},{9,15},{10,... | collective-permute-start | bytes 393224 | tf_op jit(solution)/shard_map/ppermute | solution.py:38
  345.0 6.2 %collective-permute-start.30 = (f32[128,128]{0,1:T(8,128)S(1)}, f32[128,128]{0,1:T(8,128)S(1)}, u32[]{:S(2)}, u32[]{:S(2)}) collective-permute-start(f32[128,128]{0,1:T(8,128)S(1)} %copy.45), channel_id=1, source_target_pairs={{0,32},{8,40},{16,48},{24,56},{32,64},{40,72},{48,80},{56,88},{64,... | collective-permute-start | bytes 196616 | tf_op jit(solution)/shard_map/ppermute | solution.py:31
  345.3 6.0 %collective-permute-start.31 = (f32[128,128]{0,1:T(8,128)S(1)}, f32[128,128]{0,1:T(8,128)S(1)}, u32[]{:S(2)}, u32[]{:S(2)}) collective-permute-start(f32[128,128]{0,1:T(8,128)S(1)} %copy.45), channel_id=1, source_target_pairs={{0,64},{8,72},{16,80},{24,88},{32,96},{40,104},{48,112},{56,120},{... | collective-permute-start | bytes 196616 | tf_op jit(solution)/shard_map/ppermute | solution.py:31
  346.5 5.6 %collective-permute-start.32 = (f32[128,128]{0,1:T(8,128)S(1)}, f32[128,128]{0,1:T(8,128)S(1)}, u32[]{:S(2)}, u32[]{:S(2)}) collective-permute-start(f32[128,128]{0,1:T(8,128)S(1)} %copy.45), channel_id=1, source_target_pairs={{0,96},{8,104},{16,112},{24,120},{32,0},{40,8},{48,16},{56,24},{64... | collective-permute-start | bytes 196616 | tf_op jit(solution)/shard_map/ppermute | solution.py:31
  352.1 5.5 %collective-permute-start.33 = (f32[128,128]{0,1:T(8,128)S(1)}, f32[128,128]{0,1:T(8,128)S(1)}, u32[]{:S(2)}, u32[]{:S(2)}) collective-permute-start(f32[128,128]{0,1:T(8,128)S(1)} %add_add_fusion.2), channel_id=1, source_target_pairs={{0,8},{8,16},{16,24},{24,0},{32,40},{40,48},{48,56},{56,32},{64,72... | collective-permute-start | bytes 196616 | tf_op jit(solution)/shard_map/ppermute | solution.py:31
  353.8 5.8 %collective-permute-start.34 = (f32[128,128]{0,1:T(8,128)S(1)}, f32[128,128]{0,1:T(8,128)S(1)}, u32[]{:S(2)}, u32[]{:S(2)}) collective-permute-start(f32[128,128]{0,1:T(8,128)S(1)} %add_add_fusion.2), channel_id=1, source_target_pairs={{0,16},{8,24},{16,0},{24,8},{32,48},{40,56},{48,32},{56,40},{64,80... | collective-permute-start | bytes 196616 | tf_op jit(solution)/shard_map/ppermute | solution.py:31
  355.1 4.5 collective-permute-start.35
  359.6 5.5 %collective-permute-start.36 = (f32[128,128]{0,1:T(8,128)S(1)}, f32[128,128]{0,1:T(8,128)S(1)}, u32[]{:S(2)}, u32[]{:S(2)}) collective-permute-start(f32[128,128]{0,1:T(8,128)S(1)} %add_add_fusion.1), channel_id=1, source_target_pairs={{0,2},{1,3},{2,4},{3,5},{4,6},{5,7},{6,0},{7,1},{8,10},{9,11},{10,... | collective-permute-start | bytes 196616 | tf_op jit(solution)/shard_map/ppermute | solution.py:38
  360.4 6.0 %collective-permute-start.37 = (f32[128,128]{0,1:T(8,128)S(1)}, f32[128,128]{0,1:T(8,128)S(1)}, u32[]{:S(2)}, u32[]{:S(2)}) collective-permute-start(f32[128,128]{0,1:T(8,128)S(1)} %add_add_fusion.1), channel_id=1, source_target_pairs={{0,4},{1,5},{2,6},{3,7},{4,0},{5,1},{6,2},{7,3},{8,12},{9,13},{10,... | collective-permute-start | bytes 196616 | tf_op jit(solution)/shard_map/ppermute | solution.py:38
  363.4 4.3 collective-permute-start.38
  367.7 1.5 collective-permute-start.39
  435.9 1.6 collective-permute-start.40
  438.4 10.6 %copy-start.6 = (f32[272,128]{1,0:T(8,128)}, f32[272,128]{1,0:T(8,128)S(1)}, u32[]{:S(2)}) copy-start(f32[272,128]{1,0:T(8,128)S(1)} %add.116.first) | copy-start | bytes 417796
  438.4 10.0 %collective-permute-start.41 = (f32[272,128]{1,0:T(8,128)S(1)}, f32[272,128]{1,0:T(8,128)S(1)}, u32[]{:S(2)}, u32[]{:S(2)}) collective-permute-start(f32[272,128]{1,0:T(8,128)S(1)} %add.116.first), channel_id=1, source_target_pairs={{0,2},{1,3},{2,4},{3,5},{4,6},{5,7},{6,0},{7,1},{8,10},{9,11},{10,... | collective-permute-start | bytes 417800 | tf_op jit(solution)/shard_map/ppermute | solution.py:38
  438.8 9.6 %collective-permute-start.42 = (f32[272,128]{1,0:T(8,128)S(1)}, f32[272,128]{1,0:T(8,128)S(1)}, u32[]{:S(2)}, u32[]{:S(2)}) collective-permute-start(f32[272,128]{1,0:T(8,128)S(1)} %add.116.first), channel_id=1, source_target_pairs={{0,4},{1,5},{2,6},{3,7},{4,0},{5,1},{6,2},{7,3},{8,12},{9,13},{10,... | collective-permute-start | bytes 417800 | tf_op jit(solution)/shard_map/ppermute | solution.py:38
  441.6 7.4 %collective-permute-start.43 = (f32[272,128]{1,0:T(8,128)S(1)}, f32[272,128]{1,0:T(8,128)S(1)}, u32[]{:S(2)}, u32[]{:S(2)}) collective-permute-start(f32[272,128]{1,0:T(8,128)S(1)} %add.116.first), channel_id=1, source_target_pairs={{0,6},{1,7},{2,0},{3,1},{4,2},{5,3},{6,4},{7,5},{8,14},{9,15},{10,... | collective-permute-start | bytes 417800 | tf_op jit(solution)/shard_map/ppermute | solution.py:38
  (14 other events, 12.3 us)

commit v2 on v1

--- a/solution.py
+++ b/solution.py
@@ -1,3 +1,6 @@
+import functools
+import math
+
 import jax
 import jax.numpy as jnp
 from jax import lax
@@ -8,6 +11,7 @@
 ROUNDS = 2
 SHARPNESS = 48.0
 EPS = 1e-06
+CLOSE = 1e-05
 
 SIDE = 4
 BF = jnp.bfloat16
@@ -36,16 +40,6 @@
         (y * 2 + c, (y + dy) % SIDE * 2 + (c + dc) % 2) for y in range(SIDE) for c in range(2)
     ]
     return lax.ppermute(value, "col", pairs)
-
-
-def sum_row(value):
-    value = value + shift_row(value, 1, 0) + shift_row(value, 2, 0) + shift_row(value, 3, 0)
-    return value + shift_row(value, 0, 1) + shift_row(value, 0, 2) + shift_row(value, 0, 3)
-
-
-def sum_col(value):
-    value = value + shift_col(value, 1, 0) + shift_col(value, 2, 0) + shift_col(value, 3, 0)
-    return value + shift_col(value, 0, 1)
 
 
 def whole(shape):
@@ -130,13 +124,20 @@
     )(meta, weights, *panels, tiles)
 
 
-def reduce_first_body(parts, out):
-    out[...] = jnp.sum(parts[...].astype(F32), axis=0).astype(BF)
-
-
-def reduce_down_body(parts, inverse, out):
+def share_wide(total, out, gram):
+    factor = total.astype(BF)
+    for copy in range(out.shape[0]):
+        out[copy] = factor
+    gram[...] = dot(factor, factor, (1, 1))
+
+
+def reduce_first_body(parts, out, gram):
+    share_wide(jnp.sum(parts[...].astype(F32), axis=0), out, gram)
+
+
+def reduce_down_body(parts, upper, out, gram):
     total = jnp.sum(parts[...].astype(F32), axis=0)
-    out[...] = dot(inverse[...], total, (1, 0), HIGHEST).astype(BF)
+    share_wide(dot(upper[...], total, (0, 0), HIGHEST), out, gram)
 
 
 def fold_body(where, keep, got, own, one, two, three):
@@ -147,103 +148,153 @@
         out[...] = (keep[to] + got[to]).astype(BF)
 
 
-def reduce_up_body(own, one, two, three, inverse, out):
+def reduce_up_body(own, one, two, three, upper, out, gram):
     total = own[...] + one[...].astype(F32) + two[...].astype(F32) + three[...].astype(F32)
-    out[...] = dot(total, inverse[...], (1, 1), HIGHEST).astype(BF)
-
-
-def reduce_last_body(own, one, two, three, inverse, out, gram):
+    panel = dot(total, upper[...], (1, 0), HIGHEST).astype(BF)
+    out[...] = panel
+    gram[...] = dot(panel, panel, (0, 0))
+
+
+def reduce_last_body(own, one, two, three, upper, out, gram):
     total = own[...] + one[...].astype(F32) + two[...].astype(F32) + three[...].astype(F32)
-    total = dot(total, inverse[...], (1, 1), HIGHEST)
+    total = dot(total, upper[...], (1, 0), HIGHEST)
     out[...] = total
     gram[...] = dot(total, total, (0, 0), HIGHEST)
 
 
-def gram_wide_body(parts, out):
-    total = jnp.zeros(out.shape, F32)
-    for part in range(parts.shape[0]):
-        total += dot(parts[part], parts[part], (1, 1))
-    out[...] = total
-
-
-def gram_tall_body(mine, theirs, out):
-    total = jnp.zeros(out.shape, F32)
-    for part in range(mine.shape[0]):
-        total += dot(mine[part], mine[part], (0, 0))
-        total += dot(theirs[part], theirs[part], (0, 0))
-    out[...] = total
-
-
-def inverse_factor(gram, total_rows):
-    lower = jnp.linalg.cholesky(gram / total_rows)
-    identity = jnp.eye(gram.shape[0], dtype=F32)
-    return lax.linalg.triangular_solve(lower, identity, left_side=True, lower=True)
-
-
-def cluster_body(product, inverse, centroids, panel, sums, totals, norms):
+def factor_body(total_rows, *refs):
+    *grams, out, work, build = refs
+    gram = sum(part[...] for part in grams) / total_rows
+    size = gram.shape[0]
+    down = lax.broadcasted_iota(jnp.int32, (size, size), 0)
+    across = lax.broadcasted_iota(jnp.int32, (size, size), 1)
+    eye = jnp.where(down == across, 1.0, 0.0).astype(F32)
+    keep = jnp.where(down < across, 1.0, 0.5 * eye)
+    diagonal = gram * eye
+    tall = lax.rsqrt(jnp.sum(diagonal, axis=1, keepdims=True))
+    scaled = gram * tall * lax.rsqrt(jnp.sum(diagonal, axis=0, keepdims=True))
+    build[...] = eye - keep * (scaled - eye)
+
+    def refine(state):
+        at, _ = state
+        guess = build[...]
+        excess = dot(guess, dot(scaled, guess, (1, 0), HIGHEST), (0, 0), HIGHEST) - eye
+        build[...] = guess - dot(guess, keep * excess, (1, 0), HIGHEST)
+        return at + 1, jnp.max(jnp.abs(excess))
+
+    def unfinished(state):
+        at, error = state
+        return (at < 10) & jnp.logical_not(error < CLOSE)
+
+    _, error = lax.while_loop(unfinished, refine, (jnp.int32(0), jnp.float32(1.0)))
+    out[...] = build[...] * tall
+
+    @pl.when(jnp.logical_not(error < CLOSE))
+    def _():
+        work[...] = gram
+        build[...] = eye
+
+        def eliminate(k, carry):
+            row = work[pl.ds(k, 1), :]
+            pivot = jnp.sum(jnp.where(across[:1] == k, row, 0.0), axis=1, keepdims=True)
+            column = jnp.sum(jnp.where(across == k, work[...], 0.0), axis=1, keepdims=True)
+            ratio = jnp.where(down[:, :1] > k, column / pivot, 0.0)
+            unit = build[pl.ds(k, 1), :]
+            work[...] = work[...] - ratio * row
+            build[...] = build[...] - ratio * unit
+            return carry
+
+        lax.fori_loop(0, size, eliminate, 0)
+        pivots = jnp.sum(work[...] * eye, axis=1, keepdims=True)
+        out[...] = jnp.transpose(build[...] * lax.rsqrt(pivots))
+
+
+def ring_sum(value, shift):
+    return value + shift(value, 1) + shift(value, 2) + shift(value, 3)
+
+
+def sum_x(value):
+    return ring_sum(value, lambda v, d: shift_row(v, d, 0))
+
+
+def sum_z(value):
+    return ring_sum(value, lambda v, d: shift_row(v, 0, d))
+
+
+def sum_y(value):
+    return ring_sum(value, lambda v, d: shift_col(v, d, 0))
+
+
+def factor_of(total_rows, *grams):
+    gram = grams[0]
+    return pl.pallas_call(
+        functools.partial(factor_body, total_rows),
+        out_shape=jax.ShapeDtypeStruct(gram.shape, F32),
+        scratch_shapes=[pltpu.VMEM(gram.shape, F32)] * 2,
+        name="factor",
+    )(*grams)
+
+
+def cluster_body(product, upper, centroids, panel, packed, sums, totals, norms):
     step = pl.program_id(0)
+    unit = SHARPNESS * math.log2(math.e)
 
     @pl.when(step == 0)
     def _():
         values = centroids[...].astype(F32)
-        norms[...] = jnp.sum(values * values, axis=1, keepdims=True)
+        norms[...] = unit * jnp.sum(values * values, axis=1, keepdims=True)
         sums[...] = jnp.zeros_like(sums)
         totals[...] = jnp.zeros_like(totals)
 
-    rows = dot(product[...], inverse[...], (1, 1), HIGHEST).astype(BF)
+    rows = dot(product[...], upper[...], (1, 0), HIGHEST).astype(BF)
     panel[...] = rows
     values = rows.astype(F32)
     length = jnp.sqrt(jnp.sum(values * values, axis=1, keepdims=True) + EPS)
     points = (values / length).astype(BF)
-    affinity = dot(centroids[...], points, (1, 1))
-    scores = SHARPNESS * (2.0 * affinity - norms[...])
-    shifted = jnp.exp(scores - jnp.max(scores, axis=0, keepdims=True))
-    resp = (shifted / jnp.sum(shifted, axis=0, keepdims=True)).astype(BF)
+    scores = (2.0 * unit) * dot(centroids[...], points, (1, 1)) - norms[...]
+    shifted = jnp.exp2(scores - jnp.max(scores, axis=0, keepdims=True))
+    resp = (shifted * (1.0 / jnp.sum(shifted, axis=0, keepdims=True))).astype(BF)
     sums[...] += dot(resp, points, (1, 0))
     totals[...] += dot(jnp.ones((8, resp.shape[1]), BF), resp, (1, 1))
 
-
-def cluster(product, inverse, centroids, chunk):
+    @pl.when(step == pl.num_programs(0) - 1)
+    def _():
+        share = sums.shape[0] // packed.shape[0]
+        lanes = sums.shape[1]
+        count = share // lanes
+        for piece in range(packed.shape[0]):
+            at = piece * share
+            packed[piece, :share, :] = sums[at : at + share, :].astype(BF)
+            mass = jnp.concatenate(
+                [totals[0:1, at + k * lanes : at + (k + 1) * lanes] for k in range(count)], axis=0
+            )
+            high = mass.astype(BF).astype(F32)
+            blank = jnp.zeros((16 - 2 * count, lanes), F32)
+            tail = jnp.concatenate([high, mass - high, blank], axis=0)
+            packed[piece, share:, :] = tail.astype(BF)
+
+
+def cluster(product, upper, centroids, pieces, chunk):
     rows, rank = product.shape
     count = centroids.shape[0]
+    parcel = (pieces, count // pieces + 16, rank)
     return pl.pallas_call(
         cluster_body,
         grid=(rows // chunk,),
         in_specs=[
             pl.BlockSpec((chunk, rank), lambda i: (i, 0)),
-            whole(inverse.shape),
+            whole(upper.shape),
             whole(centroids.shape),
         ],
-        out_specs=[
-            pl.BlockSpec((chunk, rank), lambda i: (i, 0)),
-            whole((count, rank)),
-            whole((8, count)),
+        out_specs=[pl.BlockSpec((chunk, rank), lambda i: (i, 0)), whole(parcel)],
+        out_shape=[jax.ShapeDtypeStruct((rows, rank), BF), jax.ShapeDtypeStruct(parcel, BF)],
+        scratch_shapes=[
+            pltpu.VMEM((count, rank), F32),
+            pltpu.VMEM((8, count), F32),
+            pltpu.VMEM((count, 1), F32),
         ],
-        out_shape=[
-            jax.ShapeDtypeStruct((rows, rank), BF),
-            jax.ShapeDtypeStruct((count, rank), F32),
-            jax.ShapeDtypeStruct((8, count), F32),
-        ],
-        scratch_shapes=[pltpu.VMEM((count, 1), F32)],
         name="cluster",
-    )(product, inverse, centroids)
-
-
-def pack_body(sums, totals, out):
-    share = sums.shape[0] // out.shape[0]
-    lanes = sums.shape[1]
-    for piece in range(out.shape[0]):
-        out[piece, :share, :] = sums[piece * share : (piece + 1) * share, :].astype(BF)
-        ends = [
-            totals[0:1, piece * share + k * lanes : piece * share + (k + 1) * lanes]
-            for k in range(share // lanes)
-        ]
-        value = jnp.concatenate(ends, axis=0)
-        high = value.astype(BF).astype(F32)
-        tail = jnp.concatenate(
-            [high, value - high, jnp.zeros((16 - 2 * len(ends), lanes), F32)], axis=0
-        )
-        out[piece, share:, :] = tail.astype(BF)
+    )(product, upper, centroids)
 
 
 def gathered_sum_body(parts, out):
@@ -298,32 +349,41 @@
     square = jax.ShapeDtypeStruct((rank, rank), F32)
     tall = jax.ShapeDtypeStruct((piece, rank), BF)
     tall_f32 = jax.ShapeDtypeStruct((piece, rank), F32)
-    wide = jax.ShapeDtypeStruct((rank, piece), BF)
     smem = pl.BlockSpec(memory_space=pltpu.SMEM)
     vmem = pl.BlockSpec(memory_space=pltpu.VMEM)
 
+    copies_shape = jax.ShapeDtypeStruct((rows_axis, rank, piece), BF)
     panel = panel_start
-    inverse = None
+    gram = None
     for round_index in range(ROUNDS):
         mine = jnp.stack([panel] + [shift_col(panel, d, 0) for d in (1, 2, 3)])
         theirs = shift_col(mine, 0, 1)
-        if round_index > 0:
-            gram = sum_row(small_call(gram_tall_body, "gram_tall", square, mine, theirs))
-            inverse = inverse_factor(gram, total_rows)
+        if gram is not None:
+            theirs, gram = lax.optimization_barrier((theirs, sum_x(gram)))
+            gram = sum_z(gram)
         (partial,) = tile_call(
             down_body, "down", meta, weights, [mine, theirs], tiles,
             [jax.ShapeDtypeStruct((rows_axis, rank, piece), BF)],
             [pltpu.VMEM((col_blocks, rank, block_size), F32), pltpu.VMEM((block_size, rank), BF)],
         )
-        parts = lax.all_to_all(partial, "row", 0, 0, tiled=True)
-        if inverse is None:
-            factor = small_call(reduce_first_body, "reduce_first", wide, parts)
+        if gram is None:
+            parts = lax.all_to_all(partial, "row", 0, 0, tiled=True)
+            copies, gram = small_call(
+                reduce_first_body, "reduce_first", [copies_shape, square], parts
+            )
         else:
-            factor = small_call(reduce_down_body, "reduce_down", wide, parts, inverse)
-        copies = jnp.broadcast_to(factor[None], (rows_axis,) + factor.shape)
+            partial, gram = lax.optimization_barrier((partial, gram))
+            parts = lax.all_to_all(partial, "row", 0, 0, tiled=True)
+            gram = sum_y(gram)
+            upper = factor_of(total_rows, gram, shift_col(gram, 0, 1))
+            copies, gram = small_call(
+                reduce_down_body, "reduce_down", [copies_shape, square], parts, upper
+            )
         gathered = lax.all_to_all(copies, "row", 0, 0, tiled=True)
-        gram = sum_col(small_call(gram_wide_body, "gram_wide", square, gathered))
-        inverse = inverse_factor(gram, total_rows)
+        gram = sum_y(gram)
+        gram = sum_x(gram + shift_col(gram, 0, 1))
+        gathered, gram = lax.optimization_barrier((gathered, gram))
+        gram = sum_z(gram)
         keep, send = tile_call(
             up_body, "up", meta, weights, [gathered], tiles,
             [jax.ShapeDtypeStruct((SIDE, piece, rank), F32)] * 2,
@@ -336,21 +396,21 @@
             out_shape=[tall_f32, tall, tall, tall],
             name="fold",
         )(where, keep, got)
+        gram, own = lax.optimization_barrier((gram, own))
+        upper = factor_of(total_rows, gram)
         one, two, three = shift_col(one, 1, 0), shift_col(two, 2, 0), shift_col(three, 3, 0)
-        if round_index + 1 < ROUNDS:
-            panel = small_call(reduce_up_body, "reduce_up", tall, own, one, two, three, inverse)
-        else:
-            product, gram = small_call(
-                reduce_last_body, "reduce_last", [tall_f32, square], own, one, two, three, inverse
-            )
-    inverse = inverse_factor(sum_col(sum_row(gram)), total_rows)
-
-    panel, sums, totals = cluster(product, inverse, centroids, 256)
+        last = round_index + 1 == ROUNDS
+        panel, gram = small_call(
+            reduce_last_body if last else reduce_up_body,
+            "reduce_last" if last else "reduce_up",
+            [tall_f32 if last else tall, square], own, one, two, three, upper,
+        )
+    gram = sum_y(sum_z(sum_x(gram)))
+    upper = factor_of(total_rows, gram, shift_col(gram, 0, 1))
+
     count = centroids.shape[0]
     share = count // rows_axis
-    packed = small_call(
-        pack_body, "pack", jax.ShapeDtypeStruct((rows_axis, share + 16, rank), BF), sums, totals
-    )
+    panel, packed = cluster(panel, upper, centroids, rows_axis, 256)
     parts = lax.all_to_all(packed, "row", 0, 0, tiled=True)
     mass = small_call(
         gathered_sum_body, "mass", jax.ShapeDtypeStruct((share + 16, rank), F32), parts

time: 479 us -> 392 us (0.82); the launches traced: 474 us -> 392 us
  other arithmetic: 98.2 us -> 9.69 us
  blocking collectives: 142 us -> 79.3 us
  Pallas kernels: 71.6 us -> 104 us
  starting transfers between devices: 73 us -> 100 us
  waiting for transfers between devices: 67.4 us -> 82.9 us
    another operation x20 -> x0, other arithmetic: 91.4 us -> none  [the longest x12 49.6 us: inverse_factor(): lower = jnp.linalg.cholesky(gram / total_rows)]
    all_to_all x2 -> x0, blocking collectives: 59.3 us -> none  [shards(): gathered = lax.all_to_all(copies, 'row', 0, 0, tiled=True)]
    pallas_call x0 -> x4, Pallas kernels: none -> 32.3 us  [factor_of(): pl.pallas_call(functools.partial(factor_body, total_rows), out_shape=jax....]
    ppermute x12 -> x24, starting transfers between devices: 21.1 us -> 36.4 us  [shift_row(): return lax.ppermute(value, 'row', pairs)]
    all_to_all x1, waiting for transfers between devices: 0.01 us -> 14 us  [shards(): parts = lax.all_to_all(partial, 'row', 0, 0, tiled=True)]
    pallas_call x9 -> x5, Pallas kernels: 23.4 us -> 14.2 us  [small_call(): return pl.pallas_call(body, out_shape=out_shapes, name=name)(*args)]
    pallas_call x4, Pallas kernels: 29.7 us -> 38.3 us  [tile_call(): pl.pallas_call(body, grid_spec=grid_spec, out_shape=outs, name=name, cost...]
    all_to_all x0 -> x2, starting transfers between devices: none -> 7.7 us  [shards(): gathered = lax.all_to_all(copies, 'row', 0, 0, tiled=True)]
  transfers between devices with their start and end apart: 45 -> 63, of which waited for: 26 -> 37; matrix products, arithmetic and copies ran while one was open for 16% -> 2% of each run, Pallas kernels for 4% -> 11%
where the time goes in v2:
time: 392 us
  Pallas kernels  104 us (27%)
  starting transfers between devices  100 us (26%)
  waiting for transfers between devices  82.9 us (21%)
  blocking collectives  79.3 us (20%)
  local copies, waits for them, and re-layouts  15.1 us (4%)
  other arithmetic  9.69 us (2%)
    ppermute x36, starting transfers between devices, shift_col(): return lax.ppermute(value, 'col', pairs)  50.8 us
    pallas_call x4, Pallas kernels, tile_call(): pl.pallas_call(body, grid_spec=grid_spec, out_shape=outs, name=name, cost...  38.3 us
    ppermute x36, waiting for transfers between devices, shift_col(): return lax.ppermute(value, 'col', pairs)  36.8 us
    ppermute x24, starting transfers between devices, shift_row(): return lax.ppermute(value, 'row', pairs)  36.4 us
    all_to_all x1, blocking collectives, shards(): parts = lax.all_to_all(partial, 'row', 0, 0, tiled=True)  35.3 us
    pallas_call x4, Pallas kernels, factor_of(): pl.pallas_call(functools.partial(factor_body, total_rows), out_shape=jax....  32.3 us
    ppermute x24, waiting for transfers between devices, shift_row(): return lax.ppermute(value, 'row', pairs)  31.5 us
    all_to_all x1, blocking collectives, shards(): parts = lax.all_to_all(packed, 'row', 0, 0, tiled=True)  24.2 us
  transfers between devices with their start and end apart: 63, of which 37 were waited for; matrix products, arithmetic and copies ran while one was open for 2% of the time, Pallas kernels for 11%

profile of v2, /device:TPU:0, one launch (start us, length us, event | category | flops | bytes accessed | tf_op | source)
XLA Modules:
  0.0 392.3 jit_solution(14776594806016598007)
XLA Ops:
  2.4 2.9 collective-permute-start.1
  7.5 4.0 %collective-permute-done.1 = bf16[512,128]{1,0:T(8,128)(2,1)S(1)} collective-permute-done((bf16[512,128]{1,0:T(8,128)(2,1)}, bf16[512,128]{1,0:T(8,128)(2,1)S(1)}, u32[]{:S(2)}, u32[]{:S(2)}) %collective-permute-start.1) | collective-permute-done | bytes 131104 | tf_op jit(solution)/shard_map/ppermute | solution.py:42
  16.9 9.2 %down.2 = bf16[16,128,512]{2,1,0:T(8,128)(2,1)} custom-call(s32[15]{0:T(128)} %concatenate.3.meta, f32[6]{0:T(128)} %select_reduce_fusion.weights, bf16[4,512,128]{2,1,0:T(8,128)(2,1)} %copy-done.3, bf16[4,512,128]{2,1,0:T(8,128)(2,1)} %copy-done.8, bf16[6,1024,1024]{2,1,0:T(8,128)(2,1)} %tile.7), custom_call_target="tpu_custom_call" | custom-call | flops 1610612736 | bytes 16777216 | tf_op jit(solution)/shard_map/down/pallas_call | solution.py:114
  26.1 35.3 %all_to_all.30.parts = bf16[16,128,512]{2,1,0:T(8,128)(2,1)} all-to-all(bf16[16,128,512]{2,1,0:T(8,128)(2,1)} %down.2), channel_id=1, replica_groups=mesh['row'=16,'col'=8] {'row'}, dimensions={0} | all-to-all | bytes 4194304 | tf_op jit(solution)/shard_map/all_to_all | solution.py:370
  61.4 3.3 reduce_first.1
  64.7 3.9 all-to-all-start.1
  68.7 5.0 %collective-permute-start.5 = (f32[128,128]{1,0:T(8,128)S(1)}, f32[128,128]{1,0:T(8,128)S(1)}, u32[]{:S(2)}, u32[]{:S(2)}) collective-permute-start(f32[128,128]{1,0:T(8,128)S(1)} %copy-done.22), channel_id=1, source_target_pairs={{0,4},{1,5},{2,6},{3,7},{4,0},{5,1},{6,2},{7,3},{8,12},{9,13},{10,... | collective-permute-start | bytes 196616 | tf_op jit(solution)/shard_map/ppermute | solution.py:42
  73.6 2.5 collective-permute-start.6
  79.4 3.2 collective-permute-start.10
  84.9 8.7 %collective-permute-done.10 = f32[128,128]{1,0:T(8,128)S(1)} collective-permute-done((f32[128,128]{1,0:T(8,128)S(1)}, f32[128,128]{1,0:T(8,128)S(1)}, u32[]{:S(2)}, u32[]{:S(2)}) %collective-permute-start.10) | collective-permute-done | bytes 65568 | tf_op jit(solution)/shard_map/ppermute | solution.py:35
  93.5 2.5 collective-permute-done.9
  97.6 10.0 %up.2 = (f32[4,512,128]{2,1,0:T(8,128)}, f32[4,512,128]{2,1,0:T(8,128)}) custom-call(s32[15]{0:T(128)} %concatenate.3.meta, f32[6]{0:T(128)} %select_reduce_fusion.weights, bf16[16,128,512]{2,1,0:T(8,128)(2,1)} %copy-done.2, bf16[6,1024,1024]{2,1,0:T(8,128)(2,1)} %tile.7), custom_call_target="tpu_custom_call" | custom-call | flops 1610612736 | bytes 16777216 | tf_op jit(solution)/shard_map/up/pallas_call | solution.py:114
  107.7 3.1 collective-permute-start.13
  111.8 2.5 fold.2
  114.3 7.4 %collective-permute-start.16 = (bf16[512,128]{1,0:T(8,128)(2,1)}, bf16[512,128]{1,0:T(8,128)(2,1)S(1)}, u32[]{:S(2)}, u32[]{:S(2)}) collective-permute-start(bf16[512,128]{1,0:T(8,128)(2,1)} %get-tuple-element.45), channel_id=1, source_target_pairs={{0,4},{1,5},{2,6},{3,7},{4,0},{5,1},{6,2},{7,3},{8,12},{9,13},{10,... | collective-permute-start | bytes 393224 | tf_op jit(solution)/shard_map/ppermute | solution.py:42
  121.7 2.6 collective-permute-start.17
  125.0 21.5 %factor.4.upper = f32[128,128]{1,0:T(8,128)} custom-call(f32[128,128]{1,0:T(8,128)} %add_add_fusion.9.refs_0_), custom_call_target="tpu_custom_call" | custom-call | tf_op jit(solution)/shard_map/factor/pallas_call | solution.py:230
  152.2 5.7 %collective-permute-done.19 = bf16[512,128]{1,0:T(8,128)(2,1)S(1)} collective-permute-done((bf16[512,128]{1,0:T(8,128)(2,1)}, bf16[512,128]{1,0:T(8,128)(2,1)S(1)}, u32[]{:S(2)}, u32[]{:S(2)}) %collective-permute-start.19) | collective-permute-done | bytes 131104 | tf_op jit(solution)/shard_map/ppermute | solution.py:42
  160.7 5.1 %collective-permute-start.23 = (f32[128,128]{1,0:T(8,128)}, f32[128,128]{1,0:T(8,128)S(1)}, u32[]{:S(2)}, u32[]{:S(2)}) collective-permute-start(f32[128,128]{1,0:T(8,128)} %get-tuple-element.49), channel_id=1, source_target_pairs={{0,64},{8,72},{16,80},{24,88},{32,96},{40,104},{48,112},{56,120},{... | collective-permute-start | bytes 196616 | tf_op jit(solution)/shard_map/ppermute | solution.py:35
  167.2 2.6 collective-permute-done.23
  174.5 9.2 %down.3 = bf16[16,128,512]{2,1,0:T(8,128)(2,1)} custom-call(s32[15]{0:T(128)} %concatenate.3.meta, f32[6]{0:T(128)} %select_reduce_fusion.weights, bf16[4,512,128]{2,1,0:T(8,128)(2,1)} %copy-done.4, bf16[4,512,128]{2,1,0:T(8,128)(2,1)} %copy-done.9, bf16[6,1024,1024]{2,1,0:T(8,128)(2,1)} %tile.7), custom_call_target="tpu_custom_call" | custom-call | flops 1610612736 | bytes 16777216 | tf_op jit(solution)/shard_map/down/pallas_call | solution.py:114
  183.7 5.2 %all-to-all-start.2 = ((bf16[16,128,512]{2,1,0:T(8,128)(2,1)}), bf16[16,128,512]{2,1,0:T(8,128)(2,1)S(1)}, u32[]{:S(2)}, u32[]{:S(2)}) async-start(bf16[16,128,512]{2,1,0:T(8,128)(2,1)} %down.3), calls=%async_computation.2 | async-start | bytes 4194304 | tf_op jit(solution)/shard_map/all_to_all | solution.py:376
  189.7 2.5 collective-permute-start.30
  192.2 2.9 collective-permute-done.28
  198.0 3.6 factor.5.upper
  201.6 14.0 %all-to-all-done.2.parts = bf16[16,128,512]{2,1,0:T(8,128)(2,1)S(1)} async-done(((bf16[16,128,512]{2,1,0:T(8,128)(2,1)}), bf16[16,128,512]{2,1,0:T(8,128)(2,1)S(1)}, u32[]{:S(2)}, u32[]{:S(2)}) %all-to-all-start.2) | async-done | bytes 2097184 | tf_op jit(solution)/shard_map/all_to_all | solution.py:376
  216.9 3.7 reduce_down.1
  220.6 3.8 all-to-all-start.3
  224.5 5.6 %collective-permute-start.33 = (f32[128,128]{1,0:T(8,128)S(1)}, f32[128,128]{1,0:T(8,128)S(1)}, u32[]{:S(2)}, u32[]{:S(2)}) collective-permute-start(f32[128,128]{1,0:T(8,128)S(1)} %copy-done.21), channel_id=1, source_target_pairs={{0,4},{1,5},{2,6},{3,7},{4,0},{5,1},{6,2},{7,3},{8,12},{9,13},{10,... | collective-permute-start | bytes 196616 | tf_op jit(solution)/shard_map/ppermute | solution.py:42
  237.8 2.7 collective-permute-start.37
  241.9 4.5 %collective-permute-done.36 = f32[128,128]{1,0:T(8,128)S(1)} collective-permute-done((f32[128,128]{1,0:T(8,128)S(1)}, f32[128,128]{1,0:T(8,128)S(1)}, u32[]{:S(2)}, u32[]{:S(2)}) %collective-permute-start.36) | collective-permute-done | bytes 65568 | tf_op jit(solution)/shard_map/ppermute | solution.py:35
  246.4 5.3 %collective-permute-done.37 = f32[128,128]{1,0:T(8,128)S(1)} collective-permute-done((f32[128,128]{1,0:T(8,128)S(1)}, f32[128,128]{1,0:T(8,128)S(1)}, u32[]{:S(2)}, u32[]{:S(2)}) %collective-permute-start.37) | collective-permute-done | bytes 65568 | tf_op jit(solution)/shard_map/ppermute | solution.py:35
  253.3 10.0 %up.3 = (f32[4,512,128]{2,1,0:T(8,128)}, f32[4,512,128]{2,1,0:T(8,128)}) custom-call(s32[15]{0:T(128)} %concatenate.3.meta, f32[6]{0:T(128)} %select_reduce_fusion.weights, bf16[16,128,512]{2,1,0:T(8,128)(2,1)} %copy-done.1, bf16[6,1024,1024]{2,1,0:T(8,128)(2,1)} %tile.7), custom_call_target="tpu_custom_call" | custom-call | flops 1610612736 | bytes 16777216 | tf_op jit(solution)/shard_map/up/pallas_call | solution.py:114
  263.4 3.1 collective-permute-start.41
  267.5 2.5 fold.3
  270.0 4.3 %collective-permute-start.44 = (bf16[512,128]{1,0:T(8,128)(2,1)}, bf16[512,128]{1,0:T(8,128)(2,1)S(1)}, u32[]{:S(2)}, u32[]{:S(2)}) collective-permute-start(bf16[512,128]{1,0:T(8,128)(2,1)} %get-tuple-element.63), channel_id=1, source_target_pairs={{0,4},{1,5},{2,6},{3,7},{4,0},{5,1},{6,2},{7,3},{8,12},{9,13},{10,... | collective-permute-start | bytes 393224 | tf_op jit(solution)/shard_map/ppermute | solution.py:42
  274.3 2.6 collective-permute-start.45
  277.6 3.7 factor.6.upper
  282.7 2.9 reduce_last.1
  286.7 3.0 collective-permute-start.47
  296.9 2.4 collective-permute-start.51
  302.6 2.5 collective-permute-start.53
  311.3 3.6 factor.7.upper
  314.9 11.8 %cluster.1 = (bf16[512,128]{1,0:T(8,128)(2,1)}, bf16[16,272,128]{2,1,0:T(8,128)(2,1)}) custom-call(f32[512,128]{1,0:T(8,128)} %get-tuple-element.66.product, f32[128,128]{1,0:T(8,128)} %factor.7.upper, bf16[4096,128]{1,0:T(8,128)(2,1)} %centroids.1), custom_call_target="tpu_custom_call" | custom-call | tf_op jit(solution)/shard_map/cluster/pallas_call | solution.py:281
  326.7 24.2 %all_to_all.31.parts = bf16[16,272,128]{2,1,0:T(8,128)(2,1)} all-to-all(bf16[16,272,128]{2,1,0:T(8,128)(2,1)} %get-tuple-element.69), channel_id=1, replica_groups=mesh['row'=16,'col'=8] {'row'}, dimensions={0} | all-to-all | bytes 2228224 | tf_op jit(solution)/shard_map/all_to_all | solution.py:414
  356.9 3.1 collective-permute-start.58
  362.6 4.2 %collective-permute-done.58.third = f32[272,128]{1,0:T(8,128)S(1)} collective-permute-done((f32[272,128]{1,0:T(8,128)S(1)}, f32[272,128]{1,0:T(8,128)S(1)}, u32[]{:S(2)}, u32[]{:S(2)}) %collective-permute-start.58) | collective-permute-done | bytes 139296 | tf_op jit(solution)/shard_map/ppermute | solution.py:42
  371.0 19.8 %all_to_all.32 = bf16[16,256,128]{2,1,0:T(8,128)(2,1)S(1)} all-to-all(bf16[16,256,128]{2,1,0:T(8,128)(2,1)S(1)} %broadcast_in_dim.24), channel_id=1, replica_groups=mesh['row'=16,'col'=8] {'row'}, dimensions={0} | all-to-all | bytes 2097152 | tf_op jit(solution)/shard_map/all_to_all | solution.py:427
  (171 shorter events, 83.2 us)
Async XLA Ops:
  0.6 6.9 %collective-permute-start = (bf16[512,128]{1,0:T(8,128)(2,1)}, bf16[512,128]{1,0:T(8,128)(2,1)S(1)}, u32[]{:S(2)}, u32[]{:S(2)}) collective-permute-start(bf16[512,128]{1,0:T(8,128)(2,1)} %param.12), channel_id=1, source_target_pairs={{0,2},{1,3},{2,4},{3,5},{4,6},{5,7},{6,0},{7,1},{8,10},{9,11},{10,... | collective-permute-start | bytes 393224 | tf_op jit(solution)/shard_map/ppermute | solution.py:42
  2.4 9.1 %collective-permute-start.1 = (bf16[512,128]{1,0:T(8,128)(2,1)}, bf16[512,128]{1,0:T(8,128)(2,1)S(1)}, u32[]{:S(2)}, u32[]{:S(2)}) collective-permute-start(bf16[512,128]{1,0:T(8,128)(2,1)} %param.12), channel_id=1, source_target_pairs={{0,4},{1,5},{2,6},{3,7},{4,0},{5,1},{6,2},{7,3},{8,12},{9,13},{10,... | collective-permute-start | bytes 393224 | tf_op jit(solution)/shard_map/ppermute | solution.py:42
  5.3 6.2 %collective-permute-start.2 = (bf16[512,128]{1,0:T(8,128)(2,1)}, bf16[512,128]{1,0:T(8,128)(2,1)S(1)}, u32[]{:S(2)}, u32[]{:S(2)}) collective-permute-start(bf16[512,128]{1,0:T(8,128)(2,1)} %param.12), channel_id=1, source_target_pairs={{0,6},{1,7},{2,0},{3,1},{4,2},{5,3},{6,4},{7,5},{8,14},{9,15},{10,... | collective-permute-start | bytes 393224 | tf_op jit(solution)/shard_map/ppermute | solution.py:42
  64.7 31.6 %all-to-all-start.1 = ((bf16[16,128,512]{2,1,0:T(8,128)(2,1)}), bf16[16,128,512]{2,1,0:T(8,128)(2,1)S(1)}, u32[]{:S(2)}, u32[]{:S(2)}) async-start(bf16[16,128,512]{2,1,0:T(8,128)(2,1)} %get-tuple-element.36), calls=%async_computation.1 | async-start | bytes 4194304 | tf_op jit(solution)/shard_map/all_to_all | solution.py:382
  68.6 7.6 %collective-permute-start.4 = (f32[128,128]{1,0:T(8,128)S(1)}, f32[128,128]{1,0:T(8,128)S(1)}, u32[]{:S(2)}, u32[]{:S(2)}) collective-permute-start(f32[128,128]{1,0:T(8,128)S(1)} %copy-done.22), channel_id=1, source_target_pairs={{0,2},{1,3},{2,4},{3,5},{4,6},{5,7},{6,0},{7,1},{8,10},{9,11},{10,... | collective-permute-start | bytes 196616 | tf_op jit(solution)/shard_map/ppermute | solution.py:42
  68.7 7.8 %collective-permute-start.5 = (f32[128,128]{1,0:T(8,128)S(1)}, f32[128,128]{1,0:T(8,128)S(1)}, u32[]{:S(2)}, u32[]{:S(2)}) collective-permute-start(f32[128,128]{1,0:T(8,128)S(1)} %copy-done.22), channel_id=1, source_target_pairs={{0,4},{1,5},{2,6},{3,7},{4,0},{5,1},{6,2},{7,3},{8,12},{9,13},{10,... | collective-permute-start | bytes 196616 | tf_op jit(solution)/shard_map/ppermute | solution.py:42
  79.4 14.1 %collective-permute-start.10 = (f32[128,128]{1,0:T(8,128)S(1)}, f32[128,128]{1,0:T(8,128)S(1)}, u32[]{:S(2)}, u32[]{:S(2)}) collective-permute-start(f32[128,128]{1,0:T(8,128)S(1)} %add.129), channel_id=1, source_target_pairs={{0,96},{8,104},{16,112},{24,120},{32,0},{40,8},{48,16},{56,24},{64... | collective-permute-start | bytes 196616 | tf_op jit(solution)/shard_map/ppermute | solution.py:35
  82.6 10.9 %collective-permute-start.8 = (f32[128,128]{1,0:T(8,128)S(1)}, f32[128,128]{1,0:T(8,128)S(1)}, u32[]{:S(2)}, u32[]{:S(2)}) collective-permute-start(f32[128,128]{1,0:T(8,128)S(1)} %add.129), channel_id=1, source_target_pairs={{0,32},{8,40},{16,48},{24,56},{32,64},{40,72},{48,80},{56,88},{64,... | collective-permute-start | bytes 196616 | tf_op jit(solution)/shard_map/ppermute | solution.py:35
  82.6 13.4 %collective-permute-start.9 = (f32[128,128]{1,0:T(8,128)S(1)}, f32[128,128]{1,0:T(8,128)S(1)}, u32[]{:S(2)}, u32[]{:S(2)}) collective-permute-start(f32[128,128]{1,0:T(8,128)S(1)} %add.129), channel_id=1, source_target_pairs={{0,64},{8,72},{16,80},{24,88},{32,96},{40,104},{48,112},{56,120},{... | collective-permute-start | bytes 196616 | tf_op jit(solution)/shard_map/ppermute | solution.py:35
  107.6 14.1 %collective-permute-start.11 = (f32[128,128]{1,0:T(8,128)S(1)}, f32[128,128]{1,0:T(8,128)S(1)}, u32[]{:S(2)}, u32[]{:S(2)}) collective-permute-start(f32[128,128]{1,0:T(8,128)S(1)} %add_add_fusion.10), channel_id=1, source_target_pairs={{0,8},{8,16},{16,24},{24,0},{32,40},{40,48},{48,56},{56,32},{64,72... | collective-permute-start | bytes 196616 | tf_op jit(solution)/shard_map/ppermute | solution.py:35
  107.6 16.7 %collective-permute-start.12 = (f32[128,128]{1,0:T(8,128)S(1)}, f32[128,128]{1,0:T(8,128)S(1)}, u32[]{:S(2)}, u32[]{:S(2)}) collective-permute-start(f32[128,128]{1,0:T(8,128)S(1)} %add_add_fusion.10), channel_id=1, source_target_pairs={{0,16},{8,24},{16,0},{24,8},{32,48},{40,56},{48,32},{56,40},{64,80... | collective-permute-start | bytes 196616 | tf_op jit(solution)/shard_map/ppermute | solution.py:35
  107.7 16.6 %collective-permute-start.13 = (f32[128,128]{1,0:T(8,128)S(1)}, f32[128,128]{1,0:T(8,128)S(1)}, u32[]{:S(2)}, u32[]{:S(2)}) collective-permute-start(f32[128,128]{1,0:T(8,128)S(1)} %add_add_fusion.10), channel_id=1, source_target_pairs={{0,24},{8,0},{16,8},{24,16},{32,56},{40,32},{48,40},{56,48},{64,88... | collective-permute-start | bytes 196616 | tf_op jit(solution)/shard_map/ppermute | solution.py:35
  114.3 32.2 %collective-permute-start.15 = (bf16[512,128]{1,0:T(8,128)(2,1)}, bf16[512,128]{1,0:T(8,128)(2,1)S(1)}, u32[]{:S(2)}, u32[]{:S(2)}) collective-permute-start(bf16[512,128]{1,0:T(8,128)(2,1)} %get-tuple-element.44), channel_id=1, source_target_pairs={{0,2},{1,3},{2,4},{3,5},{4,6},{5,7},{6,0},{7,1},{8,10},{9,11},{10,... | collective-permute-start | bytes 393224 | tf_op jit(solution)/shard_map/ppermute | solution.py:42
  114.3 32.2 %collective-permute-start.16 = (bf16[512,128]{1,0:T(8,128)(2,1)}, bf16[512,128]{1,0:T(8,128)(2,1)S(1)}, u32[]{:S(2)}, u32[]{:S(2)}) collective-permute-start(bf16[512,128]{1,0:T(8,128)(2,1)} %get-tuple-element.45), channel_id=1, source_target_pairs={{0,4},{1,5},{2,6},{3,7},{4,0},{5,1},{6,2},{7,3},{8,12},{9,13},{10,... | collective-permute-start | bytes 393224 | tf_op jit(solution)/shard_map/ppermute | solution.py:42
  121.7 24.8 %collective-permute-start.17 = (bf16[512,128]{1,0:T(8,128)(2,1)}, bf16[512,128]{1,0:T(8,128)(2,1)S(1)}, u32[]{:S(2)}, u32[]{:S(2)}) collective-permute-start(bf16[512,128]{1,0:T(8,128)(2,1)} %get-tuple-element.46), channel_id=1, source_target_pairs={{0,6},{1,7},{2,0},{3,1},{4,2},{5,3},{6,4},{7,5},{8,14},{9,15},{10,... | collective-permute-start | bytes 393224 | tf_op jit(solution)/shard_map/ppermute | solution.py:42
  150.2 7.8 %collective-permute-start.19 = (bf16[512,128]{1,0:T(8,128)(2,1)}, bf16[512,128]{1,0:T(8,128)(2,1)S(1)}, u32[]{:S(2)}, u32[]{:S(2)}) collective-permute-start(bf16[512,128]{1,0:T(8,128)(2,1)} %get-tuple-element.48), channel_id=1, source_target_pairs={{0,4},{1,5},{2,6},{3,7},{4,0},{5,1},{6,2},{7,3},{8,12},{9,13},{10,... | collective-permute-start | bytes 393224 | tf_op jit(solution)/shard_map/ppermute | solution.py:42
  150.2 7.8 %collective-permute-start.20 = (bf16[512,128]{1,0:T(8,128)(2,1)}, bf16[512,128]{1,0:T(8,128)(2,1)S(1)}, u32[]{:S(2)}, u32[]{:S(2)}) collective-permute-start(bf16[512,128]{1,0:T(8,128)(2,1)} %get-tuple-element.48), channel_id=1, source_target_pairs={{0,6},{1,7},{2,0},{3,1},{4,2},{5,3},{6,4},{7,5},{8,14},{9,15},{10,... | collective-permute-start | bytes 393224 | tf_op jit(solution)/shard_map/ppermute | solution.py:42
  152.2 7.1 %collective-permute-start.18 = (bf16[512,128]{1,0:T(8,128)(2,1)}, bf16[512,128]{1,0:T(8,128)(2,1)S(1)}, u32[]{:S(2)}, u32[]{:S(2)}) collective-permute-start(bf16[512,128]{1,0:T(8,128)(2,1)} %get-tuple-element.48), channel_id=1, source_target_pairs={{0,2},{1,3},{2,4},{3,5},{4,6},{5,7},{6,0},{7,1},{8,10},{9,11},{10,... | collective-permute-start | bytes 393224 | tf_op jit(solution)/shard_map/ppermute | solution.py:42
  160.3 10.8 %collective-permute-start.21 = (bf16[4,512,128]{2,1,0:T(8,128)(2,1)S(1)}, bf16[4,512,128]{2,1,0:T(8,128)(2,1)S(1)}, u32[]{:S(2)}, u32[]{:S(2)}) collective-permute-start(bf16[4,512,128]{2,1,0:T(8,128)(2,1)S(1)} %pad_maximum_fusion.1.mine), channel_id=1, source_target_pairs={{0,1},{1,0},{2,3},{3,2},{4,5},{5,4},{6,7},{7,6},{8,9},{9,8},{10,11... | collective-permute-start | bytes 1572872 | tf_op jit(solution)/shard_map/ppermute | solution.py:42
  160.4 6.8 %collective-permute-start.22 = (f32[128,128]{1,0:T(8,128)}, f32[128,128]{1,0:T(8,128)S(1)}, u32[]{:S(2)}, u32[]{:S(2)}) collective-permute-start(f32[128,128]{1,0:T(8,128)} %get-tuple-element.49), channel_id=1, source_target_pairs={{0,32},{8,40},{16,48},{24,56},{32,64},{40,72},{48,80},{56,88},{64,... | collective-permute-start | bytes 196616 | tf_op jit(solution)/shard_map/ppermute | solution.py:35
  160.7 9.1 %collective-permute-start.23 = (f32[128,128]{1,0:T(8,128)}, f32[128,128]{1,0:T(8,128)S(1)}, u32[]{:S(2)}, u32[]{:S(2)}) collective-permute-start(f32[128,128]{1,0:T(8,128)} %get-tuple-element.49), channel_id=1, source_target_pairs={{0,64},{8,72},{16,80},{24,88},{32,96},{40,104},{48,112},{56,120},{... | collective-permute-start | bytes 196616 | tf_op jit(solution)/shard_map/ppermute | solution.py:35
  171.1 12.6 %collective-permute-start.25 = (f32[128,128]{1,0:T(8,128)S(1)}, f32[128,128]{1,0:T(8,128)S(1)}, u32[]{:S(2)}, u32[]{:S(2)}) collective-permute-start(f32[128,128]{1,0:T(8,128)S(1)} %add_add_fusion.8), channel_id=1, source_target_pairs={{0,8},{8,16},{16,24},{24,0},{32,40},{40,48},{48,56},{56,32},{64,72... | collective-permute-start | bytes 196616 | tf_op jit(solution)/shard_map/ppermute | solution.py:35
  171.2 12.5 %collective-permute-start.26 = (f32[128,128]{1,0:T(8,128)S(1)}, f32[128,128]{1,0:T(8,128)S(1)}, u32[]{:S(2)}, u32[]{:S(2)}) collective-permute-start(f32[128,128]{1,0:T(8,128)S(1)} %add_add_fusion.8), channel_id=1, source_target_pairs={{0,16},{8,24},{16,0},{24,8},{32,48},{40,56},{48,32},{56,40},{64,80... | collective-permute-start | bytes 196616 | tf_op jit(solution)/shard_map/ppermute | solution.py:35
  172.6 11.1 %collective-permute-start.27 = (f32[128,128]{1,0:T(8,128)S(1)}, f32[128,128]{1,0:T(8,128)S(1)}, u32[]{:S(2)}, u32[]{:S(2)}) collective-permute-start(f32[128,128]{1,0:T(8,128)S(1)} %add_add_fusion.8), channel_id=1, source_target_pairs={{0,24},{8,0},{16,8},{24,16},{32,56},{40,32},{48,40},{56,48},{64,88... | collective-permute-start | bytes 196616 | tf_op jit(solution)/shard_map/ppermute | solution.py:35
  183.7 31.8 %all-to-all-start.2 = ((bf16[16,128,512]{2,1,0:T(8,128)(2,1)}), bf16[16,128,512]{2,1,0:T(8,128)(2,1)S(1)}, u32[]{:S(2)}, u32[]{:S(2)}) async-start(bf16[16,128,512]{2,1,0:T(8,128)(2,1)} %down.3), calls=%async_computation.2 | async-start | bytes 4194304 | tf_op jit(solution)/shard_map/all_to_all | solution.py:376
  188.9 6.2 %collective-permute-start.28 = (f32[128,128]{1,0:T(8,128)S(1)}, f32[128,128]{1,0:T(8,128)S(1)}, u32[]{:S(2)}, u32[]{:S(2)}) collective-permute-start(f32[128,128]{1,0:T(8,128)S(1)} %add_add_fusion.7), channel_id=1, source_target_pairs={{0,2},{1,3},{2,4},{3,5},{4,6},{5,7},{6,0},{7,1},{8,10},{9,11},{10,... | collective-permute-start | bytes 196616 | tf_op jit(solution)/shard_map/ppermute | solution.py:42
  189.0 6.2 %collective-permute-start.29 = (f32[128,128]{1,0:T(8,128)S(1)}, f32[128,128]{1,0:T(8,128)S(1)}, u32[]{:S(2)}, u32[]{:S(2)}) collective-permute-start(f32[128,128]{1,0:T(8,128)S(1)} %add_add_fusion.7), channel_id=1, source_target_pairs={{0,4},{1,5},{2,6},{3,7},{4,0},{5,1},{6,2},{7,3},{8,12},{9,13},{10,... | collective-permute-start | bytes 196616 | tf_op jit(solution)/shard_map/ppermute | solution.py:42
  189.7 6.3 %collective-permute-start.30 = (f32[128,128]{1,0:T(8,128)S(1)}, f32[128,128]{1,0:T(8,128)S(1)}, u32[]{:S(2)}, u32[]{:S(2)}) collective-permute-start(f32[128,128]{1,0:T(8,128)S(1)} %add_add_fusion.7), channel_id=1, source_target_pairs={{0,6},{1,7},{2,0},{3,1},{4,2},{5,3},{6,4},{7,5},{8,14},{9,15},{10,... | collective-permute-start | bytes 196616 | tf_op jit(solution)/shard_map/ppermute | solution.py:42
  220.6 31.5 %all-to-all-start.3 = ((bf16[16,128,512]{2,1,0:T(8,128)(2,1)}), bf16[16,128,512]{2,1,0:T(8,128)(2,1)S(1)}, u32[]{:S(2)}, u32[]{:S(2)}) async-start(bf16[16,128,512]{2,1,0:T(8,128)(2,1)} %get-tuple-element.54), calls=%async_computation.3 | async-start | bytes 4194304 | tf_op jit(solution)/shard_map/all_to_all | solution.py:382
  224.4 7.2 %collective-permute-start.32 = (f32[128,128]{1,0:T(8,128)S(1)}, f32[128,128]{1,0:T(8,128)S(1)}, u32[]{:S(2)}, u32[]{:S(2)}) collective-permute-start(f32[128,128]{1,0:T(8,128)S(1)} %copy-done.21), channel_id=1, source_target_pairs={{0,2},{1,3},{2,4},{3,5},{4,6},{5,7},{6,0},{7,1},{8,10},{9,11},{10,... | collective-permute-start | bytes 196616 | tf_op jit(solution)/shard_map/ppermute | solution.py:42
  224.5 8.6 %collective-permute-start.33 = (f32[128,128]{1,0:T(8,128)S(1)}, f32[128,128]{1,0:T(8,128)S(1)}, u32[]{:S(2)}, u32[]{:S(2)}) collective-permute-start(f32[128,128]{1,0:T(8,128)S(1)} %copy-done.21), channel_id=1, source_target_pairs={{0,4},{1,5},{2,6},{3,7},{4,0},{5,1},{6,2},{7,3},{8,12},{9,13},{10,... | collective-permute-start | bytes 196616 | tf_op jit(solution)/shard_map/ppermute | solution.py:42
  235.8 10.6 %collective-permute-start.36 = (f32[128,128]{1,0:T(8,128)S(1)}, f32[128,128]{1,0:T(8,128)S(1)}, u32[]{:S(2)}, u32[]{:S(2)}) collective-permute-start(f32[128,128]{1,0:T(8,128)S(1)} %add.148), channel_id=1, source_target_pairs={{0,32},{8,40},{16,48},{24,56},{32,64},{40,72},{48,80},{56,88},{64,... | collective-permute-start | bytes 196616 | tf_op jit(solution)/shard_map/ppermute | solution.py:35
  237.8 14.0 %collective-permute-start.37 = (f32[128,128]{1,0:T(8,128)S(1)}, f32[128,128]{1,0:T(8,128)S(1)}, u32[]{:S(2)}, u32[]{:S(2)}) collective-permute-start(f32[128,128]{1,0:T(8,128)S(1)} %add.148), channel_id=1, source_target_pairs={{0,64},{8,72},{16,80},{24,88},{32,96},{40,104},{48,112},{56,120},{... | collective-permute-start | bytes 196616 | tf_op jit(solution)/shard_map/ppermute | solution.py:35
  240.4 11.3 %collective-permute-start.38 = (f32[128,128]{1,0:T(8,128)S(1)}, f32[128,128]{1,0:T(8,128)S(1)}, u32[]{:S(2)}, u32[]{:S(2)}) collective-permute-start(f32[128,128]{1,0:T(8,128)S(1)} %add.148), channel_id=1, source_target_pairs={{0,96},{8,104},{16,112},{24,120},{32,0},{40,8},{48,16},{56,24},{64... | collective-permute-start | bytes 196616 | tf_op jit(solution)/shard_map/ppermute | solution.py:35
  263.3 11.0 %collective-permute-start.39 = (f32[128,128]{1,0:T(8,128)S(1)}, f32[128,128]{1,0:T(8,128)S(1)}, u32[]{:S(2)}, u32[]{:S(2)}) collective-permute-start(f32[128,128]{1,0:T(8,128)S(1)} %add_add_fusion.4), channel_id=1, source_target_pairs={{0,8},{8,16},{16,24},{24,0},{32,40},{40,48},{48,56},{56,32},{64,72... | collective-permute-start | bytes 196616 | tf_op jit(solution)/shard_map/ppermute | solution.py:35
  263.3 13.6 %collective-permute-start.40 = (f32[128,128]{1,0:T(8,128)S(1)}, f32[128,128]{1,0:T(8,128)S(1)}, u32[]{:S(2)}, u32[]{:S(2)}) collective-permute-start(f32[128,128]{1,0:T(8,128)S(1)} %add_add_fusion.4), channel_id=1, source_target_pairs={{0,16},{8,24},{16,0},{24,8},{32,48},{40,56},{48,32},{56,40},{64,80... | collective-permute-start | bytes 196616 | tf_op jit(solution)/shard_map/ppermute | solution.py:35
  263.4 13.5 %collective-permute-start.41 = (f32[128,128]{1,0:T(8,128)S(1)}, f32[128,128]{1,0:T(8,128)S(1)}, u32[]{:S(2)}, u32[]{:S(2)}) collective-permute-start(f32[128,128]{1,0:T(8,128)S(1)} %add_add_fusion.4), channel_id=1, source_target_pairs={{0,24},{8,0},{16,8},{24,16},{32,56},{40,32},{48,40},{56,48},{64,88... | collective-permute-start | bytes 196616 | tf_op jit(solution)/shard_map/ppermute | solution.py:35
  270.0 11.3 %collective-permute-start.43 = (bf16[512,128]{1,0:T(8,128)(2,1)}, bf16[512,128]{1,0:T(8,128)(2,1)S(1)}, u32[]{:S(2)}, u32[]{:S(2)}) collective-permute-start(bf16[512,128]{1,0:T(8,128)(2,1)} %get-tuple-element.62), channel_id=1, source_target_pairs={{0,2},{1,3},{2,4},{3,5},{4,6},{5,7},{6,0},{7,1},{8,10},{9,11},{10,... | collective-permute-start | bytes 393224 | tf_op jit(solution)/shard_map/ppermute | solution.py:42
  270.0 11.3 %collective-permute-start.44 = (bf16[512,128]{1,0:T(8,128)(2,1)}, bf16[512,128]{1,0:T(8,128)(2,1)S(1)}, u32[]{:S(2)}, u32[]{:S(2)}) collective-permute-start(bf16[512,128]{1,0:T(8,128)(2,1)} %get-tuple-element.63), channel_id=1, source_target_pairs={{0,4},{1,5},{2,6},{3,7},{4,0},{5,1},{6,2},{7,3},{8,12},{9,13},{10,... | collective-permute-start | bytes 393224 | tf_op jit(solution)/shard_map/ppermute | solution.py:42
  274.3 7.0 %collective-permute-start.45 = (bf16[512,128]{1,0:T(8,128)(2,1)}, bf16[512,128]{1,0:T(8,128)(2,1)S(1)}, u32[]{:S(2)}, u32[]{:S(2)}) collective-permute-start(bf16[512,128]{1,0:T(8,128)(2,1)} %get-tuple-element.64), channel_id=1, source_target_pairs={{0,6},{1,7},{2,0},{3,1},{4,2},{5,3},{6,4},{7,5},{8,14},{9,15},{10,... | collective-permute-start | bytes 393224 | tf_op jit(solution)/shard_map/ppermute | solution.py:42
  285.5 5.8 %collective-permute-start.46 = (f32[128,128]{1,0:T(8,128)}, f32[128,128]{1,0:T(8,128)S(1)}, u32[]{:S(2)}, u32[]{:S(2)}) collective-permute-start(f32[128,128]{1,0:T(8,128)} %get-tuple-element.67), channel_id=1, source_target_pairs={{0,32},{8,40},{16,48},{24,56},{32,64},{40,72},{48,80},{56,88},{64,... | collective-permute-start | bytes 196616 | tf_op jit(solution)/shard_map/ppermute | solution.py:35
  286.7 6.1 %collective-permute-start.47 = (f32[128,128]{1,0:T(8,128)}, f32[128,128]{1,0:T(8,128)S(1)}, u32[]{:S(2)}, u32[]{:S(2)}) collective-permute-start(f32[128,128]{1,0:T(8,128)} %get-tuple-element.67), channel_id=1, source_target_pairs={{0,64},{8,72},{16,80},{24,88},{32,96},{40,104},{48,112},{56,120},{... | collective-permute-start | bytes 196616 | tf_op jit(solution)/shard_map/ppermute | solution.py:35
  295.6 5.8 %collective-permute-start.50 = (f32[128,128]{1,0:T(8,128)S(1)}, f32[128,128]{1,0:T(8,128)S(1)}, u32[]{:S(2)}, u32[]{:S(2)}) collective-permute-start(f32[128,128]{1,0:T(8,128)S(1)} %add_add_fusion.2), channel_id=1, source_target_pairs={{0,16},{8,24},{16,0},{24,8},{32,48},{40,56},{48,32},{56,40},{64,80... | collective-permute-start | bytes 196616 | tf_op jit(solution)/shard_map/ppermute | solution.py:35
  302.1 5.5 %collective-permute-start.52 = (f32[128,128]{1,0:T(8,128)S(1)}, f32[128,128]{1,0:T(8,128)S(1)}, u32[]{:S(2)}, u32[]{:S(2)}) collective-permute-start(f32[128,128]{1,0:T(8,128)S(1)} %add_add_fusion.1), channel_id=1, source_target_pairs={{0,2},{1,3},{2,4},{3,5},{4,6},{5,7},{6,0},{7,1},{8,10},{9,11},{10,... | collective-permute-start | bytes 196616 | tf_op jit(solution)/shard_map/ppermute | solution.py:42
  302.6 5.8 %collective-permute-start.53 = (f32[128,128]{1,0:T(8,128)S(1)}, f32[128,128]{1,0:T(8,128)S(1)}, u32[]{:S(2)}, u32[]{:S(2)}) collective-permute-start(f32[128,128]{1,0:T(8,128)S(1)} %add_add_fusion.1), channel_id=1, source_target_pairs={{0,4},{1,5},{2,6},{3,7},{4,0},{5,1},{6,2},{7,3},{8,12},{9,13},{10,... | collective-permute-start | bytes 196616 | tf_op jit(solution)/shard_map/ppermute | solution.py:42
  355.4 7.2 %collective-permute-start.57 = (f32[272,128]{1,0:T(8,128)S(1)}, f32[272,128]{1,0:T(8,128)S(1)}, u32[]{:S(2)}, u32[]{:S(2)}) collective-permute-start(f32[272,128]{1,0:T(8,128)S(1)} %add.164.first), channel_id=1, source_target_pairs={{0,2},{1,3},{2,4},{3,5},{4,6},{5,7},{6,0},{7,1},{8,10},{9,11},{10,... | collective-permute-start | bytes 417800 | tf_op jit(solution)/shard_map/ppermute | solution.py:42
  356.9 9.8 %collective-permute-start.58 = (f32[272,128]{1,0:T(8,128)S(1)}, f32[272,128]{1,0:T(8,128)S(1)}, u32[]{:S(2)}, u32[]{:S(2)}) collective-permute-start(f32[272,128]{1,0:T(8,128)S(1)} %add.164.first), channel_id=1, source_target_pairs={{0,4},{1,5},{2,6},{3,7},{4,0},{5,1},{6,2},{7,3},{8,12},{9,13},{10,... | collective-permute-start | bytes 417800 | tf_op jit(solution)/shard_map/ppermute | solution.py:42
  360.1 6.7 %collective-permute-start.59 = (f32[272,128]{1,0:T(8,128)S(1)}, f32[272,128]{1,0:T(8,128)S(1)}, u32[]{:S(2)}, u32[]{:S(2)}) collective-permute-start(f32[272,128]{1,0:T(8,128)S(1)} %add.164.first), channel_id=1, source_target_pairs={{0,6},{1,7},{2,0},{3,1},{4,2},{5,3},{6,4},{7,5},{8,14},{9,15},{10,... | collective-permute-start | bytes 417800 | tf_op jit(solution)/shard_map/ppermute | solution.py:42
  (40 other events, 110.1 us)

commit v3 on v2

v3 whole, which is shorter than its diff:
```python
import functools
import math

import jax
import jax.numpy as jnp
from jax import lax
from jax.experimental import pallas as pl
from jax.experimental.pallas import tpu as pltpu
from jax.sharding import PartitionSpec as P

ROUNDS = 2
SHARPNESS = 48.0
EPS = 1e-06
CLOSE = 1e-05

SIDE = 4
BF = jnp.bfloat16
F32 = jnp.float32
HIGHEST = lax.Precision.HIGHEST


def dot(a, b, contract, precision=None):
    return lax.dot_general(
        a, b, ((contract[:1], contract[1:]), ((), ())), precision=precision,
        preferred_element_type=F32,
    )


def shift_row(value, dx, dz):
    pairs = [
        (x * SIDE + z, (x + dx) % SIDE * SIDE + (z + dz) % SIDE)
        for x in range(SIDE)
        for z in range(SIDE)
    ]
    return lax.ppermute(value, "row", pairs)


def shift_col(value, dy, dc):
    pairs = [
        (y * 2 + c, (y + dy) % SIDE * 2 + (c + dc) % 2) for y in range(SIDE) for c in range(2)
    ]
    return lax.ppermute(value, "col", pairs)


def near(value):
    return pltpu.with_memory_space_constraint(value, pltpu.VMEM)


def small_call(body, out_shapes, *args, where=None, scratch=(), far=0):
    scalars = [] if where is None else [where]
    return pl.pallas_call(
        body,
        in_specs=[pl.BlockSpec(memory_space=pltpu.SMEM)] * len(scalars)
        + [pl.BlockSpec(memory_space=pltpu.VMEM)] * len(args),
        out_shape=out_shapes,
        scratch_shapes=scratch,
    )(*scalars, *args[:far], *(near(arg) for arg in args[far:]))


def each_tile(meta, tiles, buffers, arrivals, acc, add):
    def load(slot):
        return pltpu.make_async_copy(tiles.at[slot], buffers.at[slot], arrivals.at[slot])

    def start(slot, carry):
        load(slot).start()
        return carry

    def finish(slot, carry):
        load(slot).wait()
        add(slot)
        return carry

    lax.fori_loop(0, meta[12], start, 0)
    acc[...] = jnp.zeros_like(acc)
    lax.fori_loop(0, meta[12], finish, 0)


def down_body(meta, weights, mine, theirs, tiles, out, acc, rows, buffers, arrivals):
    half = mine.shape[1]
    core = meta[14]

    def add(slot):
        place = (meta[13] + SIDE - meta[slot]) % SIDE
        rows[pl.ds(pl.multiple_of(core * half, half), half), :] = mine[place]
        rows[pl.ds(pl.multiple_of((1 - core) * half, half), half), :] = theirs[place]
        product = dot(rows[...], buffers[slot], (0, 0))
        target = meta[6 + slot]
        acc[target] = acc[target] + weights[slot] * product

    each_tile(meta, tiles, buffers, arrivals, acc, add)
    for block in range(acc.shape[0]):
        out[2 * block] = acc[block, :, :half].astype(BF)
        out[2 * block + 1] = acc[block, :, half:].astype(BF)


def up_body(meta, weights, gathered, tiles, keep, send, acc, buffers, arrivals):
    half = gathered.shape[2]
    core = meta[14]

    def add(slot):
        source = meta[6 + slot]
        product = dot(buffers[slot, :, :half], gathered[2 * source], (1, 1))
        product += dot(buffers[slot, :, half:], gathered[2 * source + 1], (1, 1))
        target = meta[slot]
        acc[target] = acc[target] + weights[slot] * product

    each_tile(meta, tiles, buffers, arrivals, acc, add)
    for block in range(acc.shape[0]):
        keep[block] = acc[block, pl.ds(pl.multiple_of(core * half, half), half), :]
        send[block] = acc[block, pl.ds(pl.multiple_of((1 - core) * half, half), half), :]


def tile_call(body, meta, weights, panels, tiles, outs, scratch):
    slots, block, _ = tiles.shape
    return pl.pallas_call(
        body,
        in_specs=[pl.BlockSpec(memory_space=pltpu.SMEM)] * 2
        + [pl.BlockSpec(memory_space=pltpu.VMEM)] * len(panels)
        + [pl.BlockSpec(memory_space=pl.ANY)],
        out_shape=outs,
        scratch_shapes=scratch
        + [pltpu.VMEM(tiles.shape, BF), pltpu.SemaphoreType.DMA((slots,))],
        cost_estimate=pl.CostEstimate(
            flops=2 * slots * block * block * 128,
            transcendentals=0,
            bytes_accessed=slots * block * block * 2 + 4 * 1024 * 1024,
        ),
    )(meta, weights, *(near(panel) for panel in panels), tiles)


def share_wide(total, out, gram):
    factor = total.astype(BF)
    for copy in range(out.shape[0]):
        out[copy] = factor
    gram[...] = dot(factor, factor, (1, 1))


def reduce_first_body(parts, out, gram):
    share_wide(jnp.sum(parts[...].astype(F32), axis=0), out, gram)


def reduce_down_body(parts, upper, out, gram):
    total = jnp.sum(parts[...].astype(F32), axis=0)
    share_wide(dot(upper[...], total, (0, 0), HIGHEST), out, gram)


def fold_body(where, keep, got, own, one, two, three):
    at = where[0]
    own[...] = keep[at] + got[at]
    for distance, out in ((1, one), (2, two), (3, three)):
        to = (at + distance) % SIDE
        out[...] = (keep[to] + got[to]).astype(BF)


def reduce_up_body(own, one, two, three, upper, out, gram):
    total = own[...] + one[...].astype(F32) + two[...].astype(F32) + three[...].astype(F32)
    panel = dot(total, upper[...], (1, 0), HIGHEST).astype(BF)
    out[...] = panel
    gram[...] = dot(panel, panel, (0, 0))


def reduce_last_body(own, one, two, three, upper, out, gram):
    total = own[...] + one[...].astype(F32) + two[...].astype(F32) + three[...].astype(F32)
    total = dot(total, upper[...], (1, 0), HIGHEST)
    out[...] = total
    gram[...] = dot(total, total, (0, 0), HIGHEST)


def factor_body(total_rows, *refs):
    *grams, out, work, build = refs
    gram = sum(part[...] for part in grams) / total_rows
    size = gram.shape[0]
    down = lax.broadcasted_iota(jnp.int32, (size, size), 0)
    across = lax.broadcasted_iota(jnp.int32, (size, size), 1)
    eye = jnp.where(down == across, 1.0, 0.0).astype(F32)
    keep = jnp.where(down < across, 1.0, 0.5 * eye)
    diagonal = gram * eye
    tall = lax.rsqrt(jnp.sum(diagonal, axis=1, keepdims=True))
    scaled = gram * tall * lax.rsqrt(jnp.sum(diagonal, axis=0, keepdims=True))
    build[...] = eye - keep * (scaled - eye)

    def refine(state):
        at, _ = state
        guess = build[...]
        excess = dot(guess, dot(scaled, guess, (1, 0), HIGHEST), (0, 0), HIGHEST) - eye
        build[...] = guess - dot(guess, keep * excess, (1, 0), HIGHEST)
        return at + 1, jnp.max(jnp.abs(excess))

    def unfinished(state):
        at, error = state
        return (at < 10) & jnp.logical_not(error < CLOSE)

    _, error = lax.while_loop(unfinished, refine, (jnp.int32(0), jnp.float32(1.0)))
    out[...] = build[...] * tall

    @pl.when(jnp.logical_not(error < CLOSE))
    def _():
        work[...] = gram
        build[...] = eye

        def eliminate(k, carry):
            row = work[pl.ds(k, 1), :]
            pivot = jnp.sum(jnp.where(across[:1] == k, row, 0.0), axis=1, keepdims=True)
            column = jnp.sum(jnp.where(across == k, work[...], 0.0), axis=1, keepdims=True)
            ratio = jnp.where(down[:, :1] > k, column / pivot, 0.0)
            unit = build[pl.ds(k, 1), :]
            work[...] = work[...] - ratio * row
            build[...] = build[...] - ratio * unit
            return carry

        lax.fori_loop(0, size, eliminate, 0)
        pivots = jnp.sum(work[...] * eye, axis=1, keepdims=True)
        out[...] = jnp.transpose(build[...] * lax.rsqrt(pivots))


def ring(value, shift):
    return [value] + [shift(value, d) for d in (1, 2, 3)]


def ring_sum(value, shift):
    return sum(ring(value, shift))


def sum_x(value):
    return ring_sum(value, lambda v, d: shift_row(v, d, 0))


def sum_z(value):
    return ring_sum(value, lambda v, d: shift_row(v, 0, d))


def sum_y(value):
    return ring_sum(value, lambda v, d: shift_col(v, d, 0))


def factor_of(total_rows, *grams):
    gram = grams[0]
    return small_call(
        functools.partial(factor_body, total_rows),
        pltpu.VMEM(gram.shape, F32), *grams,
        scratch=[pltpu.VMEM(gram.shape, F32)] * 2,
    )


def cluster_body(where, product, upper, centroids, panel, keep, send, sums, totals, norms):
    step = pl.program_id(0)
    unit = SHARPNESS * math.log2(math.e)
    lanes = sums.shape[1]

    @pl.when(step == 0)
    def _():
        values = centroids[...].astype(F32)
        norms[...] = unit * jnp.sum(values * values, axis=1, keepdims=True)
        sums[...] = jnp.zeros_like(sums)
        totals[...] = jnp.zeros_like(totals)

    rows = dot(product[...], upper[...], (1, 0), HIGHEST).astype(BF)
    panel[...] = rows
    values = rows.astype(F32)
    length = jnp.sqrt(jnp.sum(values * values, axis=1, keepdims=True) + EPS)
    points = (values / length).astype(BF)
    scores = (2.0 * unit) * dot(centroids[...], points, (1, 1)) - norms[...]
    shifted = jnp.exp2(scores - jnp.max(scores, axis=0, keepdims=True))
    resp = (shifted * (1.0 / jnp.sum(shifted, axis=0, keepdims=True))).astype(BF)
    sums[...] += dot(resp, points, (1, 0))
    ones = jnp.ones((8, resp.shape[1]), BF)
    for block in range(totals.shape[0]):
        totals[block] += dot(ones, resp[block * lanes : (block + 1) * lanes], (1, 1))

    @pl.when(step == pl.num_programs(0) - 1)
    def _():
        core = where[1]
        blank = jnp.zeros((14, lanes), F32)
        for piece in range(keep.shape[0]):
            block = core * keep.shape[0] + piece
            keep[piece, :lanes, :] = sums[pl.ds(pl.multiple_of(block * lanes, lanes), lanes), :]
            keep[piece, lanes:, :] = jnp.concatenate(
                [totals[block, 0:1], jnp.zeros((1, lanes), F32), blank], axis=0
            )
            block = (1 - core) * keep.shape[0] + piece
            out = sums[pl.ds(pl.multiple_of(block * lanes, lanes), lanes), :]
            send[piece, :lanes, :] = out.astype(BF)
            send[piece, lanes:, :] = pair(totals[block, 0:1]).astype(BF)


def pair(mass):
    high = mass.astype(BF).astype(F32)
    return jnp.concatenate([high, mass - high, jnp.zeros((14, mass.shape[1]), F32)], axis=0)


def cluster(where, product, upper, centroids, pieces, chunk):
    rows, rank = product.shape
    count = centroids.shape[0]
    parcel = (pieces, rank + 16, rank)
    return pl.pallas_call(
        cluster_body,
        grid=(rows // chunk,),
        in_specs=[
            pl.BlockSpec(memory_space=pltpu.SMEM),
            pl.BlockSpec((chunk, rank), lambda i: (i, 0)),
            pl.BlockSpec(memory_space=pltpu.VMEM),
            pl.BlockSpec((count, rank), lambda i: (0, 0)),
        ],
        out_specs=[
            pl.BlockSpec((chunk, rank), lambda i: (i, 0)),
            pl.BlockSpec(parcel, lambda i: (0, 0, 0)),
            pl.BlockSpec(parcel, lambda i: (0, 0, 0)),
        ],
        out_shape=[
            jax.ShapeDtypeStruct((rows, rank), BF),
            jax.ShapeDtypeStruct(parcel, F32),
            jax.ShapeDtypeStruct(parcel, BF),
        ],
        scratch_shapes=[
            pltpu.VMEM((count, rank), F32),
            pltpu.VMEM((count // rank, 8, rank), F32),
            pltpu.VMEM((count, 1), F32),
        ],
        name="cluster",
    )(where, product, near(upper), centroids)


def pool_body(keep, got, out):
    lanes = out.shape[2]
    out[:, :lanes, :] = (keep[:, :lanes, :] + got[:, :lanes, :].astype(F32)).astype(BF)
    for piece in range(out.shape[0]):
        tail = got[piece, lanes:, :].astype(F32)
        mass = keep[piece, lanes : lanes + 1, :] + tail[0:1] + tail[1:2]
        out[piece, lanes:, :] = pair(mass).astype(BF)


def mass_body(parts, out):
    lanes = out.shape[1]
    total = jnp.sum(parts[...].astype(F32), axis=0)
    out[:lanes, :] = total[:lanes]
    out[lanes:, :] = jnp.broadcast_to(total[lanes : lanes + 1] + total[lanes + 1 : lanes + 2], (8, lanes))


def centers_body(where, first, second, third, fourth, centroids, out):
    stack = [part[...] for part in (first, second, third, fourth)]
    lanes = out.shape[2]
    total = jnp.zeros_like(stack[0])
    for y in range(SIDE):
        place = (where[0] + SIDE - y) % SIDE
        pick = stack[0]
        for k in range(1, SIDE):
            pick = jnp.where(place == k, stack[k], pick)
        total = total + pick
    column = jnp.transpose(jnp.broadcast_to(total[lanes : lanes + 1], (lanes, lanes)))
    values = ((total[:lanes] + centroids[...].astype(F32)) / (column + 1.0)).astype(BF)
    for copy in range(out.shape[0]):
        out[copy] = values


def centers_of(where, masses, centroids, pieces):
    lanes = centroids.shape[1]
    near_spec = pl.BlockSpec(memory_space=pltpu.VMEM)
    return pl.pallas_call(
        centers_body,
        grid_spec=pltpu.PrefetchScalarGridSpec(
            num_scalar_prefetch=1,
            grid=(1,),
            in_specs=[near_spec] * len(masses)
            + [pl.BlockSpec((lanes, lanes), lambda i, at: (at[1] * pieces + at[2], 0))],
            out_specs=pl.BlockSpec((pieces, lanes, lanes), lambda i, at: (0, 0, 0)),
        ),
        out_shape=jax.ShapeDtypeStruct((pieces, lanes, lanes), BF),
        name="centers",
    )(where, *(near(mass) for mass in masses), centroids)


def join_body(where, mine, theirs, out):
    core = where[1]
    lanes = out.shape[2]
    for piece in range(mine.shape[0]):
        rows = slice(piece * lanes, (piece + 1) * lanes)
        out[core, rows, :] = mine[piece].astype(F32)
        out[1 - core, rows, :] = theirs[piece].astype(F32)


def shards(tiles, tile_list, tile_count, scale_index, scales, panel_start, centroids):
    block_size = tiles.shape[1]
    piece, rank = panel_start.shape
    rows_axis = lax.axis_size("row")
    cols_axis = lax.axis_size("col")
    total_rows = piece * rows_axis * cols_axis
    row_at = lax.axis_index("row")
    col_at = lax.axis_index("col")
    row_blocks = piece * cols_axis // block_size
    col_blocks = piece * rows_axis // block_size
    meta = jnp.concatenate(
        [
            tile_list[:, 0] - row_at * row_blocks,
            tile_list[:, 1] - col_at * col_blocks,
            tile_count,
            jnp.stack([col_at // 2, col_at % 2]).astype(jnp.int32),
        ]
    )
    where = jnp.stack([col_at // 2, col_at % 2, row_at]).astype(jnp.int32)
    table_ids = jnp.arange(scales.shape[0], dtype=jnp.int32)
    weights = jnp.sum(
        jnp.where(scale_index[:, None] == table_ids[None, :], scales[None, :], 0.0), axis=1
    )
    spot = pltpu.VMEM
    square = spot((rank, rank), F32)
    tall = spot((piece, rank), BF)
    tall_f32 = spot((piece, rank), F32)

    copies_shape = jax.ShapeDtypeStruct((rows_axis, rank, piece), BF)
    panel = panel_start
    gram = None
    for round_index in range(ROUNDS):
        last = round_index + 1 == ROUNDS
        shifted = [shift_col(panel, d, 0) for d in (1, 2, 3)]
        if gram is not None:
            *shifted, gram = lax.optimization_barrier((*shifted, sum_x(gram)))
            gram = sum_z(gram)
        mine = jnp.stack([panel] + shifted)
        theirs = shift_col(mine, 0, 1)
        partial = tile_call(
            down_body, meta, weights, [mine, theirs], tiles, copies_shape,
            [pltpu.VMEM((col_blocks, rank, block_size), F32), pltpu.VMEM((block_size, rank), BF)],
        )
        if gram is None:
            parts = lax.all_to_all(partial, "row", 0, 0, tiled=True)
            copies, gram = small_call(reduce_first_body, [copies_shape, square], parts)
        else:
            partial, gram = lax.optimization_barrier((partial, gram))
            parts = lax.all_to_all(partial, "row", 0, 0, tiled=True)
            gram = sum_y(gram)
            upper = factor_of(total_rows, gram, shift_col(gram, 0, 1))
            copies, gram = small_call(reduce_down_body, [copies_shape, square], parts, upper)
        gathered = lax.all_to_all(copies, "row", 0, 0, tiled=True)
        gram = sum_y(gram)
        gram = sum_x(gram + shift_col(gram, 0, 1))
        gathered, gram = lax.optimization_barrier((gathered, gram))
        grams = ring(gram, lambda v, d: shift_row(v, 0, d))
        keep, send = tile_call(
            up_body, meta, weights, [gathered], tiles,
            [jax.ShapeDtypeStruct((SIDE, piece, rank), F32)] * 2,
            [pltpu.VMEM((row_blocks, block_size, rank), F32)],
        )
        got = shift_col(send, 0, 1)
        own, one, two, three = small_call(
            fold_body, [tall_f32, tall, tall, tall], keep, got, where=where,
            far=1,
        )
        *grams, own = lax.optimization_barrier((*grams, own))
        upper = factor_of(total_rows, *grams)
        one, two, three = shift_col(one, 1, 0), shift_col(two, 2, 0), shift_col(three, 3, 0)
        panel, gram = small_call(
            reduce_last_body if last else reduce_up_body,
            [tall_f32 if last else tall, square], own, one, two, three, upper,
        )
    gram = sum_y(gram + shift_col(gram, 0, 1))
    upper = factor_of(total_rows, *ring(sum_x(gram), lambda v, d: shift_row(v, 0, d)))

    panel, keep, send = cluster(where, panel, upper, centroids, rows_axis, 256)
    got = shift_col(send, 0, 1)
    packed = small_call(pool_body, spot(send.shape, BF), keep, got, far=1)
    parts = lax.all_to_all(packed, "row", 0, 0, tiled=True)
    mass = small_call(mass_body, spot((rank + 8, rank), F32), parts)
    masses = [mass] + [shift_col(mass, d, 0) for d in (1, 2, 3)]
    copies = centers_of(where, masses, centroids, rows_axis)
    mine = lax.all_to_all(copies, "row", 0, 0, tiled=True)
    theirs = shift_col(mine, 0, 1)
    count = centroids.shape[0]
    centers = small_call(
        join_body, jax.ShapeDtypeStruct((2, count // 2, rank), F32), mine, theirs,
        where=where,
    )
    return (panel, centers.reshape(count, rank))


def solution(mesh):
    return jax.shard_map(
        shards,
        mesh=mesh,
        in_specs=(
            P(("row", "col"), None, None),
            P(("row", "col"), None),
            P(("row", "col")),
            P(("row", "col")),
            P(),
            P(("row", "col"), None),
            P(),
        ),
        out_specs=(P(("row", "col"), None), P()),
        check_vma=False,
    )
```

time: 392 us -> 358 us (0.913)
  Pallas kernels: 104 us -> 70.4 us
  waiting for transfers between devices: 82.9 us -> 114 us
  local copies, waits for them, and re-layouts: 15.1 us -> 3.54 us
  blocking collectives: 79.3 us -> 67.9 us
  other arithmetic: 9.69 us -> 3.95 us
  starting transfers between devices: 100 us -> 94.4 us
    pallas_call x16 -> x18, Pallas kernels: 91.7 us -> 58.3 us  [the longest x13 38.2 us: small_call(): pl.pallas_call(body, in_specs=[pl.BlockSpec(memory_space=pltpu.SMEM)] * l...]
    ppermute x24, waiting for transfers between devices: 31.5 us -> 50.4 us  [shift_row(): return lax.ppermute(value, 'row', pairs)]
    unnamed x50 -> x6, local copies, waits for them, and re-layouts: 11.9 us -> 2.91 us
    all_to_all x1, blocking collectives: 24.2 us -> 16.3 us  [shards(): parts = lax.all_to_all(packed, 'row', 0, 0, tiled=True)]
    ppermute x36 -> x37, waiting for transfers between devices: 36.8 us -> 44.4 us  [shift_col(): return lax.ppermute(value, 'col', pairs)]
    all_to_all x1, blocking collectives: 19.8 us -> 13.6 us  [shards(): mine = lax.all_to_all(copies, 'row', 0, 0, tiled=True)]
    ppermute x36 -> x37, starting transfers between devices: 50.8 us -> 45.2 us  [shift_col(): return lax.ppermute(value, 'col', pairs)]
  transfers between devices with their start and end apart: 63 -> 64, of which waited for: 37 -> 50; matrix products, arithmetic and copies ran while one was open for 2% -> 1% of each run, Pallas kernels for 11% -> 8%
where the time goes in v3:
time: 358 us; the launch traced here: 356 us
  waiting for transfers between devices  114 us (32%)
  starting transfers between devices  94.4 us (26%)
  Pallas kernels  70.4 us (20%)
  blocking collectives  67.9 us (19%)
  other arithmetic  3.95 us (1%)
    ppermute x24, waiting for transfers between devices, shift_row(): return lax.ppermute(value, 'row', pairs)  50.4 us
    ppermute x37, starting transfers between devices, shift_col(): return lax.ppermute(value, 'col', pairs)  45.2 us
    ppermute x37, waiting for transfers between devices, shift_col(): return lax.ppermute(value, 'col', pairs)  44.4 us
    pallas_call x13, Pallas kernels, small_call(): pl.pallas_call(body, in_specs=[pl.BlockSpec(memory_space=pltpu.SMEM)] * l...  38.2 us
    all_to_all x1, blocking collectives, shards(): parts = lax.all_to_all(partial, 'row', 0, 0, tiled=True)  38 us
    ppermute x24, starting transfers between devices, shift_row(): return lax.ppermute(value, 'row', pairs)  34.4 us
    pallas_call x4, Pallas kernels, tile_call(): pl.pallas_call(body, in_specs=[pl.BlockSpec(memory_space=pltpu.SMEM)] * 2...  17.7 us
    all_to_all x1, waiting for transfers between devices, shards(): parts = lax.all_to_all(partial, 'row', 0, 0, tiled=True)  16.9 us
  transfers between devices with their start and end apart: 64, of which 50 were waited for; matrix products, arithmetic and copies ran while one was open for 1% of the time, Pallas kernels for 8%

profile of v3, /device:TPU:0, one launch (start us, length us, event | category | flops | bytes accessed | tf_op | source)
XLA Modules:
  0.0 356.3 jit_solution(184089089689964198)
XLA Ops:
  3.9 2.1 collective-permute-start.1
  7.5 2.3 collective-permute-done.2
  16.0 4.3 %shard_map.86 = bf16[16,128,512]{2,1,0:T(8,128)(2,1)} custom-call(s32[15]{0:T(128)} %concatenate.3.meta, f32[6]{0:T(128)} %select_reduce_fusion.weights, bf16[4,512,128]{2,1,0:T(8,128)(2,1)S(1)} %pad_maximum_fusion.mine, bf16[4,512,128]{2,1,0:T(8,128)(2,1)S(1)} %collective-permute-done.3.theirs, bf16[6,1024,1024]{2,1,0:T(8,128)(2,1)} %tiles.7), custom_call_target="tpu_custom_call" | custom-call | flops 1610612736 | bytes 16777216 | tf_op jit(solution)/shard_map/pallas_call | solution.py:115
  20.4 38.0 %all_to_all.30.parts = bf16[16,128,512]{2,1,0:T(8,128)(2,1)S(1)} all-to-all(bf16[16,128,512]{2,1,0:T(8,128)(2,1)} %shard_map.86), channel_id=1, replica_groups=mesh['row'=16,'col'=8] {'row'}, dimensions={0} | all-to-all | bytes 4194304 | tf_op jit(solution)/shard_map/all_to_all | solution.py:425
  60.1 3.7 %all-to-all-start.1 = ((bf16[16,128,512]{2,1,0:T(8,128)(2,1)}), bf16[16,128,512]{2,1,0:T(8,128)(2,1)S(1)}, u32[]{:S(2)}, u32[]{:S(2)}) async-start(bf16[16,128,512]{2,1,0:T(8,128)(2,1)} %get-tuple-element.45), calls=%async_computation.1 | async-start | bytes 4194304 | tf_op jit(solution)/shard_map/all_to_all | solution.py:433
  63.8 2.2 collective-permute-start.6
  69.2 2.7 collective-permute-done.5
  73.9 3.1 collective-permute-start.10
  78.8 11.2 %collective-permute-done.10 = f32[128,128]{1,0:T(8,128)S(1)} collective-permute-done((f32[128,128]{1,0:T(8,128)S(1)}, f32[128,128]{1,0:T(8,128)S(1)}, u32[]{:S(2)}, u32[]{:S(2)}) %collective-permute-start.10) | collective-permute-done | bytes 65568 | tf_op jit(solution)/shard_map/ppermute | solution.py:35
  93.2 4.5 %shard_map.88 = (f32[4,512,128]{2,1,0:T(8,128)}, f32[4,512,128]{2,1,0:T(8,128)}) custom-call(s32[15]{0:T(128)} %concatenate.3.meta, f32[6]{0:T(128)} %select_reduce_fusion.weights, bf16[16,128,512]{2,1,0:T(8,128)(2,1)S(1)} %all-to-all-done.1.gathered, bf16[6,1024,1024]{2,1,0:T(8,128)(2,1)} %tiles.7), custom_call_target="tpu_custom_call" | custom-call | flops 1610612736 | bytes 16777216 | tf_op jit(solution)/shard_map/pallas_call | solution.py:115
  97.8 2.2 collective-permute-start.13
  102.0 3.5 collective-permute-start.15
  106.8 2.5 collective-permute-start.17
  109.3 2.5 collective-permute-start.12
  112.4 3.2 collective-permute-done.12.refs_2_
  117.3 20.0 %shard_map.90.upper = f32[128,128]{1,0:T(8,128)S(1)} custom-call(f32[128,128]{1,0:T(8,128)S(1)} %add_add_fusion.7.refs_0_, f32[128,128]{1,0:T(8,128)S(1)} %collective-permute-done.11.refs_1_, f32[128,128]{1,0:T(8,128)S(1)} %collective-permute-done.12.refs_2_, f32[128,128]{1,0:T(8,128)S(1)} %collective-permute-done.13.refs_3_), custom_call_target="tpu_custom_call" | custom-call | tf_op jit(solution)/shard_map/pallas_call | solution.py:51
  138.0 5.0 %collective-permute-start.23 = (f32[128,128]{1,0:T(8,128)S(1)}, f32[128,128]{1,0:T(8,128)S(1)}, u32[]{:S(2)}, u32[]{:S(2)}) collective-permute-start(f32[128,128]{1,0:T(8,128)S(1)} %get-tuple-element.61), channel_id=1, source_target_pairs={{0,96},{8,104},{16,112},{24,120},{32,0},{40,8},{48,16},{56,24},{64... | collective-permute-start | bytes 196616 | tf_op jit(solution)/shard_map/ppermute | solution.py:35
  146.0 2.9 collective-permute-done.22
  154.7 2.4 collective-permute-done.27
  159.5 4.4 %shard_map.92 = bf16[16,128,512]{2,1,0:T(8,128)(2,1)} custom-call(s32[15]{0:T(128)} %concatenate.3.meta, f32[6]{0:T(128)} %select_reduce_fusion.weights, bf16[4,512,128]{2,1,0:T(8,128)(2,1)S(1)} %pad_maximum_fusion.1.mine, bf16[4,512,128]{2,1,0:T(8,128)(2,1)S(1)} %collective-permute-done.24.theirs, bf16[6,1024,1024]{2,1,0:T(8,128)(2,1)} %tiles.7), custom_call_target="tpu_custom_call" | custom-call | flops 1610612736 | bytes 16777216 | tf_op jit(solution)/shard_map/pallas_call | solution.py:115
  163.9 7.2 %all-to-all-start.2 = ((bf16[16,128,512]{2,1,0:T(8,128)(2,1)}), bf16[16,128,512]{2,1,0:T(8,128)(2,1)S(1)}, u32[]{:S(2)}, u32[]{:S(2)}) async-start(bf16[16,128,512]{2,1,0:T(8,128)(2,1)} %shard_map.92), calls=%async_computation.2 | async-start | bytes 4194304 | tf_op jit(solution)/shard_map/all_to_all | solution.py:429
  172.6 2.1 collective-permute-start.29
  176.1 2.6 collective-permute-done.29
  183.6 16.9 %all-to-all-done.2.parts = bf16[16,128,512]{2,1,0:T(8,128)(2,1)S(1)} async-done(((bf16[16,128,512]{2,1,0:T(8,128)(2,1)}), bf16[16,128,512]{2,1,0:T(8,128)(2,1)S(1)}, u32[]{:S(2)}, u32[]{:S(2)}) %all-to-all-start.2) | async-done | bytes 2097184 | tf_op jit(solution)/shard_map/all_to_all | solution.py:429
  203.5 2.1 shard_map.94
  205.6 3.9 %all-to-all-start.3 = ((bf16[16,128,512]{2,1,0:T(8,128)(2,1)}), bf16[16,128,512]{2,1,0:T(8,128)(2,1)S(1)}, u32[]{:S(2)}, u32[]{:S(2)}) async-start(bf16[16,128,512]{2,1,0:T(8,128)(2,1)} %get-tuple-element.68), calls=%async_computation.3 | async-start | bytes 4194304 | tf_op jit(solution)/shard_map/all_to_all | solution.py:433
  209.5 4.0 %collective-permute-start.34 = (f32[128,128]{1,0:T(8,128)S(1)}, f32[128,128]{1,0:T(8,128)S(1)}, u32[]{:S(2)}, u32[]{:S(2)}) collective-permute-start(f32[128,128]{1,0:T(8,128)S(1)} %get-tuple-element.69), channel_id=1, source_target_pairs={{0,6},{1,7},{2,0},{3,1},{4,2},{5,3},{6,4},{7,5},{8,14},{9,15},{10,... | collective-permute-start | bytes 196616 | tf_op jit(solution)/shard_map/ppermute | solution.py:42
  216.7 2.6 collective-permute-done.33
  222.3 3.1 collective-permute-start.38
  227.1 8.1 %collective-permute-done.38 = f32[128,128]{1,0:T(8,128)S(1)} collective-permute-done((f32[128,128]{1,0:T(8,128)S(1)}, f32[128,128]{1,0:T(8,128)S(1)}, u32[]{:S(2)}, u32[]{:S(2)}) %collective-permute-start.38) | collective-permute-done | bytes 65568 | tf_op jit(solution)/shard_map/ppermute | solution.py:35
  238.1 4.5 %shard_map.95 = (f32[4,512,128]{2,1,0:T(8,128)}, f32[4,512,128]{2,1,0:T(8,128)}) custom-call(s32[15]{0:T(128)} %concatenate.3.meta, f32[6]{0:T(128)} %select_reduce_fusion.weights, bf16[16,128,512]{2,1,0:T(8,128)(2,1)S(1)} %all-to-all-done.3.gathered, bf16[6,1024,1024]{2,1,0:T(8,128)(2,1)} %tiles.7), custom_call_target="tpu_custom_call" | custom-call | flops 1610612736 | bytes 16777216 | tf_op jit(solution)/shard_map/pallas_call | solution.py:115
  246.9 3.5 collective-permute-start.43
  250.4 4.6 %collective-permute-start.44 = (bf16[512,128]{1,0:T(8,128)(2,1)S(1)}, bf16[512,128]{1,0:T(8,128)(2,1)S(1)}, u32[]{:S(2)}, u32[]{:S(2)}) collective-permute-start(bf16[512,128]{1,0:T(8,128)(2,1)S(1)} %get-tuple-element.77), channel_id=1, source_target_pairs={{0,4},{1,5},{2,6},{3,7},{4,0},{5,1},{6,2},{7,3},{8,12},{9,13},{10,... | collective-permute-start | bytes 393224 | tf_op jit(solution)/shard_map/ppermute | solution.py:42
  255.0 2.5 collective-permute-start.45
  257.6 2.1 collective-permute-start.40
  260.2 3.2 collective-permute-done.40.refs_2_
  265.1 2.3 shard_map.97.upper
  272.0 2.8 collective-permute-done.49
  277.2 2.9 collective-permute-start.52
  282.7 3.2 collective-permute-done.51
  291.0 2.1 collective-permute-done.54.refs_2_
  295.9 12.1 %cluster.1 = (bf16[512,128]{1,0:T(8,128)(2,1)}, f32[16,144,128]{2,1,0:T(8,128)}, bf16[16,144,128]{2,1,0:T(8,128)(2,1)}) custom-call(s32[3]{0:T(128)} %pad_add_fusion.where, f32[512,128]{1,0:T(8,128)} %copy-done.2, f32[128,128]{1,0:T(8,128)S(1)} %shard_map.99.upper, bf16[4096,128]{1,0:T(8,128)(2,1)} %centroids.3), custom_call_target="tpu_custom_call" | custom-call | tf_op jit(solution)/shard_map/cluster/pallas_call | solution.py:295
  308.0 2.2 collective-permute-done.56.got
  311.6 16.3 %all_to_all.31.parts = bf16[16,144,128]{2,1,0:T(8,128)(2,1)S(1)} all-to-all(bf16[16,144,128]{2,1,0:T(8,128)(2,1)S(1)} %shard_map.100), channel_id=1, replica_groups=mesh['row'=16,'col'=8] {'row'}, dimensions={0} | all-to-all | bytes 1179648 | tf_op jit(solution)/shard_map/all_to_all | solution.py:461
  332.3 3.2 collective-permute-done.58.third
  336.3 2.4 centers.1
  338.6 13.6 %all_to_all.32.mine = bf16[16,128,128]{2,1,0:T(8,128)(2,1)S(1)} all-to-all(bf16[16,128,128]{2,1,0:T(8,128)(2,1)} %centers.1), channel_id=1, replica_groups=mesh['row'=16,'col'=8] {'row'}, dimensions={0} | all-to-all | bytes 1048576 | tf_op jit(solution)/shard_map/all_to_all | solution.py:465
  354.2 2.1 shard_map.102
  (126 shorter events, 93.4 us)
Async XLA Ops:
  0.6 6.9 %collective-permute-start = (bf16[512,128]{1,0:T(8,128)(2,1)}, bf16[512,128]{1,0:T(8,128)(2,1)S(1)}, u32[]{:S(2)}, u32[]{:S(2)}) collective-permute-start(bf16[512,128]{1,0:T(8,128)(2,1)} %param.12), channel_id=1, source_target_pairs={{0,2},{1,3},{2,4},{3,5},{4,6},{5,7},{6,0},{7,1},{8,10},{9,11},{10,... | collective-permute-start | bytes 393224 | tf_op jit(solution)/shard_map/ppermute | solution.py:42
  2.4 7.4 %collective-permute-start.2 = (bf16[512,128]{1,0:T(8,128)(2,1)}, bf16[512,128]{1,0:T(8,128)(2,1)S(1)}, u32[]{:S(2)}, u32[]{:S(2)}) collective-permute-start(bf16[512,128]{1,0:T(8,128)(2,1)} %param.12), channel_id=1, source_target_pairs={{0,6},{1,7},{2,0},{3,1},{4,2},{5,3},{6,4},{7,5},{8,14},{9,15},{10,... | collective-permute-start | bytes 393224 | tf_op jit(solution)/shard_map/ppermute | solution.py:42
  3.9 7.6 %collective-permute-start.1 = (bf16[512,128]{1,0:T(8,128)(2,1)}, bf16[512,128]{1,0:T(8,128)(2,1)S(1)}, u32[]{:S(2)}, u32[]{:S(2)}) collective-permute-start(bf16[512,128]{1,0:T(8,128)(2,1)} %param.12), channel_id=1, source_target_pairs={{0,4},{1,5},{2,6},{3,7},{4,0},{5,1},{6,2},{7,3},{8,12},{9,13},{10,... | collective-permute-start | bytes 393224 | tf_op jit(solution)/shard_map/ppermute | solution.py:42
  60.1 33.1 %all-to-all-start.1 = ((bf16[16,128,512]{2,1,0:T(8,128)(2,1)}), bf16[16,128,512]{2,1,0:T(8,128)(2,1)S(1)}, u32[]{:S(2)}, u32[]{:S(2)}) async-start(bf16[16,128,512]{2,1,0:T(8,128)(2,1)} %get-tuple-element.45), calls=%async_computation.1 | async-start | bytes 4194304 | tf_op jit(solution)/shard_map/all_to_all | solution.py:433
  66.1 5.8 %collective-permute-start.5 = (f32[128,128]{1,0:T(8,128)S(1)}, f32[128,128]{1,0:T(8,128)S(1)}, u32[]{:S(2)}, u32[]{:S(2)}) collective-permute-start(f32[128,128]{1,0:T(8,128)S(1)} %get-tuple-element.46), channel_id=1, source_target_pairs={{0,4},{1,5},{2,6},{3,7},{4,0},{5,1},{6,2},{7,3},{8,12},{9,13},{10,... | collective-permute-start | bytes 196616 | tf_op jit(solution)/shard_map/ppermute | solution.py:42
  67.0 5.5 %collective-permute-start.4 = (f32[128,128]{1,0:T(8,128)S(1)}, f32[128,128]{1,0:T(8,128)S(1)}, u32[]{:S(2)}, u32[]{:S(2)}) collective-permute-start(f32[128,128]{1,0:T(8,128)S(1)} %get-tuple-element.46), channel_id=1, source_target_pairs={{0,2},{1,3},{2,4},{3,5},{4,6},{5,7},{6,0},{7,1},{8,10},{9,11},{10,... | collective-permute-start | bytes 196616 | tf_op jit(solution)/shard_map/ppermute | solution.py:42
  73.9 16.0 %collective-permute-start.10 = (f32[128,128]{1,0:T(8,128)S(1)}, f32[128,128]{1,0:T(8,128)S(1)}, u32[]{:S(2)}, u32[]{:S(2)}) collective-permute-start(f32[128,128]{1,0:T(8,128)S(1)} %add.100), channel_id=1, source_target_pairs={{0,96},{8,104},{16,112},{24,120},{32,0},{40,8},{48,16},{56,24},{64... | collective-permute-start | bytes 196616 | tf_op jit(solution)/shard_map/ppermute | solution.py:35
  77.1 14.4 %collective-permute-start.9 = (f32[128,128]{1,0:T(8,128)S(1)}, f32[128,128]{1,0:T(8,128)S(1)}, u32[]{:S(2)}, u32[]{:S(2)}) collective-permute-start(f32[128,128]{1,0:T(8,128)S(1)} %add.100), channel_id=1, source_target_pairs={{0,64},{8,72},{16,80},{24,88},{32,96},{40,104},{48,112},{56,120},{... | collective-permute-start | bytes 196616 | tf_op jit(solution)/shard_map/ppermute | solution.py:35
  77.9 13.9 %collective-permute-start.8 = (f32[128,128]{1,0:T(8,128)S(1)}, f32[128,128]{1,0:T(8,128)S(1)}, u32[]{:S(2)}, u32[]{:S(2)}) collective-permute-start(f32[128,128]{1,0:T(8,128)S(1)} %add.100), channel_id=1, source_target_pairs={{0,32},{8,40},{16,48},{24,56},{32,64},{40,72},{48,80},{56,88},{64,... | collective-permute-start | bytes 196616 | tf_op jit(solution)/shard_map/ppermute | solution.py:35
  97.8 14.1 %collective-permute-start.13 = (f32[128,128]{1,0:T(8,128)S(1)}, f32[128,128]{1,0:T(8,128)S(1)}, u32[]{:S(2)}, u32[]{:S(2)}) collective-permute-start(f32[128,128]{1,0:T(8,128)S(1)} %add_add_fusion.7.refs_0_), channel_id=1, source_target_pairs={{0,24},{8,0},{16,8},{24,16},{32,56},{40,32},{48,40},{56,48},{64,88... | collective-permute-start | bytes 196616 | tf_op jit(solution)/shard_map/ppermute | solution.py:35
  102.0 35.4 %collective-permute-start.15 = (bf16[512,128]{1,0:T(8,128)(2,1)S(1)}, bf16[512,128]{1,0:T(8,128)(2,1)S(1)}, u32[]{:S(2)}, u32[]{:S(2)}) collective-permute-start(bf16[512,128]{1,0:T(8,128)(2,1)S(1)} %get-tuple-element.53), channel_id=1, source_target_pairs={{0,2},{1,3},{2,4},{3,5},{4,6},{5,7},{6,0},{7,1},{8,10},{9,11},{10,... | collective-permute-start | bytes 393224 | tf_op jit(solution)/shard_map/ppermute | solution.py:42
  105.5 31.9 %collective-permute-start.16 = (bf16[512,128]{1,0:T(8,128)(2,1)S(1)}, bf16[512,128]{1,0:T(8,128)(2,1)S(1)}, u32[]{:S(2)}, u32[]{:S(2)}) collective-permute-start(bf16[512,128]{1,0:T(8,128)(2,1)S(1)} %get-tuple-element.54), channel_id=1, source_target_pairs={{0,4},{1,5},{2,6},{3,7},{4,0},{5,1},{6,2},{7,3},{8,12},{9,13},{10,... | collective-permute-start | bytes 393224 | tf_op jit(solution)/shard_map/ppermute | solution.py:42
  106.8 30.6 %collective-permute-start.17 = (bf16[512,128]{1,0:T(8,128)(2,1)S(1)}, bf16[512,128]{1,0:T(8,128)(2,1)S(1)}, u32[]{:S(2)}, u32[]{:S(2)}) collective-permute-start(bf16[512,128]{1,0:T(8,128)(2,1)S(1)} %get-tuple-element.55), channel_id=1, source_target_pairs={{0,6},{1,7},{2,0},{3,1},{4,2},{5,3},{6,4},{7,5},{8,14},{9,15},{10,... | collective-permute-start | bytes 393224 | tf_op jit(solution)/shard_map/ppermute | solution.py:42
  109.3 6.2 %collective-permute-start.12 = (f32[128,128]{1,0:T(8,128)S(1)}, f32[128,128]{1,0:T(8,128)S(1)}, u32[]{:S(2)}, u32[]{:S(2)}) collective-permute-start(f32[128,128]{1,0:T(8,128)S(1)} %add_add_fusion.7.refs_0_), channel_id=1, source_target_pairs={{0,16},{8,24},{16,0},{24,8},{32,48},{40,56},{48,32},{56,40},{64,80... | collective-permute-start | bytes 196616 | tf_op jit(solution)/shard_map/ppermute | solution.py:35
  111.9 5.5 %collective-permute-start.11 = (f32[128,128]{1,0:T(8,128)S(1)}, f32[128,128]{1,0:T(8,128)S(1)}, u32[]{:S(2)}, u32[]{:S(2)}) collective-permute-start(f32[128,128]{1,0:T(8,128)S(1)} %add_add_fusion.7.refs_0_), channel_id=1, source_target_pairs={{0,8},{8,16},{16,24},{24,0},{32,40},{40,48},{48,56},{56,32},{64,72... | collective-permute-start | bytes 196616 | tf_op jit(solution)/shard_map/ppermute | solution.py:35
  138.0 7.5 %collective-permute-start.23 = (f32[128,128]{1,0:T(8,128)S(1)}, f32[128,128]{1,0:T(8,128)S(1)}, u32[]{:S(2)}, u32[]{:S(2)}) collective-permute-start(f32[128,128]{1,0:T(8,128)S(1)} %get-tuple-element.61), channel_id=1, source_target_pairs={{0,96},{8,104},{16,112},{24,120},{32,0},{40,8},{48,16},{56,24},{64... | collective-permute-start | bytes 196616 | tf_op jit(solution)/shard_map/ppermute | solution.py:35
  143.0 5.9 %collective-permute-start.22 = (f32[128,128]{1,0:T(8,128)S(1)}, f32[128,128]{1,0:T(8,128)S(1)}, u32[]{:S(2)}, u32[]{:S(2)}) collective-permute-start(f32[128,128]{1,0:T(8,128)S(1)} %get-tuple-element.61), channel_id=1, source_target_pairs={{0,64},{8,72},{16,80},{24,88},{32,96},{40,104},{48,112},{56,120},{... | collective-permute-start | bytes 196616 | tf_op jit(solution)/shard_map/ppermute | solution.py:35
  143.1 6.2 %collective-permute-start.21 = (f32[128,128]{1,0:T(8,128)S(1)}, f32[128,128]{1,0:T(8,128)S(1)}, u32[]{:S(2)}, u32[]{:S(2)}) collective-permute-start(f32[128,128]{1,0:T(8,128)S(1)} %get-tuple-element.61), channel_id=1, source_target_pairs={{0,32},{8,40},{16,48},{24,56},{32,64},{40,72},{48,80},{56,88},{64,... | collective-permute-start | bytes 196616 | tf_op jit(solution)/shard_map/ppermute | solution.py:35
  144.0 6.6 %collective-permute-start.19 = (bf16[512,128]{1,0:T(8,128)(2,1)S(1)}, bf16[512,128]{1,0:T(8,128)(2,1)S(1)}, u32[]{:S(2)}, u32[]{:S(2)}) collective-permute-start(bf16[512,128]{1,0:T(8,128)(2,1)S(1)} %get-tuple-element.60), channel_id=1, source_target_pairs={{0,4},{1,5},{2,6},{3,7},{4,0},{5,1},{6,2},{7,3},{8,12},{9,13},{10,... | collective-permute-start | bytes 393224 | tf_op jit(solution)/shard_map/ppermute | solution.py:42
  145.6 6.4 %collective-permute-start.18 = (bf16[512,128]{1,0:T(8,128)(2,1)S(1)}, bf16[512,128]{1,0:T(8,128)(2,1)S(1)}, u32[]{:S(2)}, u32[]{:S(2)}) collective-permute-start(bf16[512,128]{1,0:T(8,128)(2,1)S(1)} %get-tuple-element.60), channel_id=1, source_target_pairs={{0,2},{1,3},{2,4},{3,5},{4,6},{5,7},{6,0},{7,1},{8,10},{9,11},{10,... | collective-permute-start | bytes 393224 | tf_op jit(solution)/shard_map/ppermute | solution.py:42
  152.0 7.5 %collective-permute-start.24 = (bf16[4,512,128]{2,1,0:T(8,128)(2,1)S(1)}, bf16[4,512,128]{2,1,0:T(8,128)(2,1)S(1)}, u32[]{:S(2)}, u32[]{:S(2)}) collective-permute-start(bf16[4,512,128]{2,1,0:T(8,128)(2,1)S(1)} %pad_maximum_fusion.1.mine), channel_id=1, source_target_pairs={{0,1},{1,0},{2,3},{3,2},{4,5},{5,4},{6,7},{7,6},{8,9},{9,8},{10,11... | collective-permute-start | bytes 1572872 | tf_op jit(solution)/shard_map/ppermute | solution.py:42
  152.2 6.0 %collective-permute-start.26 = (f32[128,128]{1,0:T(8,128)S(1)}, f32[128,128]{1,0:T(8,128)S(1)}, u32[]{:S(2)}, u32[]{:S(2)}) collective-permute-start(f32[128,128]{1,0:T(8,128)S(1)} %add_add_fusion.6), channel_id=1, source_target_pairs={{0,16},{8,24},{16,0},{24,8},{32,48},{40,56},{48,32},{56,40},{64,80... | collective-permute-start | bytes 196616 | tf_op jit(solution)/shard_map/ppermute | solution.py:35
  154.0 5.5 %collective-permute-start.25 = (f32[128,128]{1,0:T(8,128)S(1)}, f32[128,128]{1,0:T(8,128)S(1)}, u32[]{:S(2)}, u32[]{:S(2)}) collective-permute-start(f32[128,128]{1,0:T(8,128)S(1)} %add_add_fusion.6), channel_id=1, source_target_pairs={{0,8},{8,16},{16,24},{24,0},{32,40},{40,48},{48,56},{56,32},{64,72... | collective-permute-start | bytes 196616 | tf_op jit(solution)/shard_map/ppermute | solution.py:35
  163.9 36.7 %all-to-all-start.2 = ((bf16[16,128,512]{2,1,0:T(8,128)(2,1)}), bf16[16,128,512]{2,1,0:T(8,128)(2,1)S(1)}, u32[]{:S(2)}, u32[]{:S(2)}) async-start(bf16[16,128,512]{2,1,0:T(8,128)(2,1)} %shard_map.92), calls=%async_computation.2 | async-start | bytes 4194304 | tf_op jit(solution)/shard_map/all_to_all | solution.py:429
  172.6 6.1 %collective-permute-start.29 = (f32[128,128]{1,0:T(8,128)S(1)}, f32[128,128]{1,0:T(8,128)S(1)}, u32[]{:S(2)}, u32[]{:S(2)}) collective-permute-start(f32[128,128]{1,0:T(8,128)S(1)} %add_add_fusion.5), channel_id=1, source_target_pairs={{0,4},{1,5},{2,6},{3,7},{4,0},{5,1},{6,2},{7,3},{8,12},{9,13},{10,... | collective-permute-start | bytes 196616 | tf_op jit(solution)/shard_map/ppermute | solution.py:42
  174.7 5.5 %collective-permute-start.28 = (f32[128,128]{1,0:T(8,128)S(1)}, f32[128,128]{1,0:T(8,128)S(1)}, u32[]{:S(2)}, u32[]{:S(2)}) collective-permute-start(f32[128,128]{1,0:T(8,128)S(1)} %add_add_fusion.5), channel_id=1, source_target_pairs={{0,2},{1,3},{2,4},{3,5},{4,6},{5,7},{6,0},{7,1},{8,10},{9,11},{10,... | collective-permute-start | bytes 196616 | tf_op jit(solution)/shard_map/ppermute | solution.py:42
  205.6 32.6 %all-to-all-start.3 = ((bf16[16,128,512]{2,1,0:T(8,128)(2,1)}), bf16[16,128,512]{2,1,0:T(8,128)(2,1)S(1)}, u32[]{:S(2)}, u32[]{:S(2)}) async-start(bf16[16,128,512]{2,1,0:T(8,128)(2,1)} %get-tuple-element.68), calls=%async_computation.3 | async-start | bytes 4194304 | tf_op jit(solution)/shard_map/all_to_all | solution.py:433
  209.5 7.2 %collective-permute-start.34 = (f32[128,128]{1,0:T(8,128)S(1)}, f32[128,128]{1,0:T(8,128)S(1)}, u32[]{:S(2)}, u32[]{:S(2)}) collective-permute-start(f32[128,128]{1,0:T(8,128)S(1)} %get-tuple-element.69), channel_id=1, source_target_pairs={{0,6},{1,7},{2,0},{3,1},{4,2},{5,3},{6,4},{7,5},{8,14},{9,15},{10,... | collective-permute-start | bytes 196616 | tf_op jit(solution)/shard_map/ppermute | solution.py:42
  213.5 5.8 %collective-permute-start.33 = (f32[128,128]{1,0:T(8,128)S(1)}, f32[128,128]{1,0:T(8,128)S(1)}, u32[]{:S(2)}, u32[]{:S(2)}) collective-permute-start(f32[128,128]{1,0:T(8,128)S(1)} %get-tuple-element.69), channel_id=1, source_target_pairs={{0,4},{1,5},{2,6},{3,7},{4,0},{5,1},{6,2},{7,3},{8,12},{9,13},{10,... | collective-permute-start | bytes 196616 | tf_op jit(solution)/shard_map/ppermute | solution.py:42
  215.4 5.5 %collective-permute-start.32 = (f32[128,128]{1,0:T(8,128)S(1)}, f32[128,128]{1,0:T(8,128)S(1)}, u32[]{:S(2)}, u32[]{:S(2)}) collective-permute-start(f32[128,128]{1,0:T(8,128)S(1)} %get-tuple-element.69), channel_id=1, source_target_pairs={{0,2},{1,3},{2,4},{3,5},{4,6},{5,7},{6,0},{7,1},{8,10},{9,11},{10,... | collective-permute-start | bytes 196616 | tf_op jit(solution)/shard_map/ppermute | solution.py:42
  222.3 12.9 %collective-permute-start.38 = (f32[128,128]{1,0:T(8,128)S(1)}, f32[128,128]{1,0:T(8,128)S(1)}, u32[]{:S(2)}, u32[]{:S(2)}) collective-permute-start(f32[128,128]{1,0:T(8,128)S(1)} %add.116), channel_id=1, source_target_pairs={{0,96},{8,104},{16,112},{24,120},{32,0},{40,8},{48,16},{56,24},{64... | collective-permute-start | bytes 196616 | tf_op jit(solution)/shard_map/ppermute | solution.py:35
  225.4 11.4 %collective-permute-start.37 = (f32[128,128]{1,0:T(8,128)S(1)}, f32[128,128]{1,0:T(8,128)S(1)}, u32[]{:S(2)}, u32[]{:S(2)}) collective-permute-start(f32[128,128]{1,0:T(8,128)S(1)} %add.116), channel_id=1, source_target_pairs={{0,64},{8,72},{16,80},{24,88},{32,96},{40,104},{48,112},{56,120},{... | collective-permute-start | bytes 196616 | tf_op jit(solution)/shard_map/ppermute | solution.py:35
  226.2 10.5 %collective-permute-start.36 = (f32[128,128]{1,0:T(8,128)S(1)}, f32[128,128]{1,0:T(8,128)S(1)}, u32[]{:S(2)}, u32[]{:S(2)}) collective-permute-start(f32[128,128]{1,0:T(8,128)S(1)} %add.116), channel_id=1, source_target_pairs={{0,32},{8,40},{16,48},{24,56},{32,64},{40,72},{48,80},{56,88},{64,... | collective-permute-start | bytes 196616 | tf_op jit(solution)/shard_map/ppermute | solution.py:35
  242.7 16.9 %collective-permute-start.41 = (f32[128,128]{1,0:T(8,128)S(1)}, f32[128,128]{1,0:T(8,128)S(1)}, u32[]{:S(2)}, u32[]{:S(2)}) collective-permute-start(f32[128,128]{1,0:T(8,128)S(1)} %add_add_fusion.2.refs_0_), channel_id=1, source_target_pairs={{0,24},{8,0},{16,8},{24,16},{32,56},{40,32},{48,40},{56,48},{64,88... | collective-permute-start | bytes 196616 | tf_op jit(solution)/shard_map/ppermute | solution.py:35
  246.9 20.5 %collective-permute-start.43 = (bf16[512,128]{1,0:T(8,128)(2,1)S(1)}, bf16[512,128]{1,0:T(8,128)(2,1)S(1)}, u32[]{:S(2)}, u32[]{:S(2)}) collective-permute-start(bf16[512,128]{1,0:T(8,128)(2,1)S(1)} %get-tuple-element.76), channel_id=1, source_target_pairs={{0,2},{1,3},{2,4},{3,5},{4,6},{5,7},{6,0},{7,1},{8,10},{9,11},{10,... | collective-permute-start | bytes 393224 | tf_op jit(solution)/shard_map/ppermute | solution.py:42
  250.4 17.0 %collective-permute-start.44 = (bf16[512,128]{1,0:T(8,128)(2,1)S(1)}, bf16[512,128]{1,0:T(8,128)(2,1)S(1)}, u32[]{:S(2)}, u32[]{:S(2)}) collective-permute-start(bf16[512,128]{1,0:T(8,128)(2,1)S(1)} %get-tuple-element.77), channel_id=1, source_target_pairs={{0,4},{1,5},{2,6},{3,7},{4,0},{5,1},{6,2},{7,3},{8,12},{9,13},{10,... | collective-permute-start | bytes 393224 | tf_op jit(solution)/shard_map/ppermute | solution.py:42
  255.0 12.4 %collective-permute-start.45 = (bf16[512,128]{1,0:T(8,128)(2,1)S(1)}, bf16[512,128]{1,0:T(8,128)(2,1)S(1)}, u32[]{:S(2)}, u32[]{:S(2)}) collective-permute-start(bf16[512,128]{1,0:T(8,128)(2,1)S(1)} %get-tuple-element.78), channel_id=1, source_target_pairs={{0,6},{1,7},{2,0},{3,1},{4,2},{5,3},{6,4},{7,5},{8,14},{9,15},{10,... | collective-permute-start | bytes 393224 | tf_op jit(solution)/shard_map/ppermute | solution.py:42
  257.6 5.9 %collective-permute-start.40 = (f32[128,128]{1,0:T(8,128)S(1)}, f32[128,128]{1,0:T(8,128)S(1)}, u32[]{:S(2)}, u32[]{:S(2)}) collective-permute-start(f32[128,128]{1,0:T(8,128)S(1)} %add_add_fusion.2.refs_0_), channel_id=1, source_target_pairs={{0,16},{8,24},{16,0},{24,8},{32,48},{40,56},{48,32},{56,40},{64,80... | collective-permute-start | bytes 196616 | tf_op jit(solution)/shard_map/ppermute | solution.py:35
  259.6 5.5 %collective-permute-start.39 = (f32[128,128]{1,0:T(8,128)S(1)}, f32[128,128]{1,0:T(8,128)S(1)}, u32[]{:S(2)}, u32[]{:S(2)}) collective-permute-start(f32[128,128]{1,0:T(8,128)S(1)} %add_add_fusion.2.refs_0_), channel_id=1, source_target_pairs={{0,8},{8,16},{16,24},{24,0},{32,40},{40,48},{48,56},{56,32},{64,72... | collective-permute-start | bytes 196616 | tf_op jit(solution)/shard_map/ppermute | solution.py:35
  270.0 6.0 %collective-permute-start.48 = (f32[128,128]{1,0:T(8,128)S(1)}, f32[128,128]{1,0:T(8,128)S(1)}, u32[]{:S(2)}, u32[]{:S(2)}) collective-permute-start(f32[128,128]{1,0:T(8,128)S(1)} %add.120), channel_id=1, source_target_pairs={{0,4},{1,5},{2,6},{3,7},{4,0},{5,1},{6,2},{7,3},{8,12},{9,13},{10,... | collective-permute-start | bytes 196616 | tf_op jit(solution)/shard_map/ppermute | solution.py:42
  271.5 5.7 %collective-permute-start.47 = (f32[128,128]{1,0:T(8,128)S(1)}, f32[128,128]{1,0:T(8,128)S(1)}, u32[]{:S(2)}, u32[]{:S(2)}) collective-permute-start(f32[128,128]{1,0:T(8,128)S(1)} %add.120), channel_id=1, source_target_pairs={{0,2},{1,3},{2,4},{3,5},{4,6},{5,7},{6,0},{7,1},{8,10},{9,11},{10,... | collective-permute-start | bytes 196616 | tf_op jit(solution)/shard_map/ppermute | solution.py:42
  277.2 5.5 %collective-permute-start.52 = (f32[128,128]{1,0:T(8,128)S(1)}, f32[128,128]{1,0:T(8,128)S(1)}, u32[]{:S(2)}, u32[]{:S(2)}) collective-permute-start(f32[128,128]{1,0:T(8,128)S(1)} %add_add_fusion.1), channel_id=1, source_target_pairs={{0,96},{8,104},{16,112},{24,120},{32,0},{40,8},{48,16},{56,24},{64... | collective-permute-start | bytes 196616 | tf_op jit(solution)/shard_map/ppermute | solution.py:35
  280.1 5.8 %collective-permute-start.51 = (f32[128,128]{1,0:T(8,128)S(1)}, f32[128,128]{1,0:T(8,128)S(1)}, u32[]{:S(2)}, u32[]{:S(2)}) collective-permute-start(f32[128,128]{1,0:T(8,128)S(1)} %add_add_fusion.1), channel_id=1, source_target_pairs={{0,64},{8,72},{16,80},{24,88},{32,96},{40,104},{48,112},{56,120},{... | collective-permute-start | bytes 196616 | tf_op jit(solution)/shard_map/ppermute | solution.py:35
  281.2 5.5 %collective-permute-start.50 = (f32[128,128]{1,0:T(8,128)S(1)}, f32[128,128]{1,0:T(8,128)S(1)}, u32[]{:S(2)}, u32[]{:S(2)}) collective-permute-start(f32[128,128]{1,0:T(8,128)S(1)} %add_add_fusion.1), channel_id=1, source_target_pairs={{0,32},{8,40},{16,48},{24,56},{32,64},{40,72},{48,80},{56,88},{64,... | collective-permute-start | bytes 196616 | tf_op jit(solution)/shard_map/ppermute | solution.py:35
  287.3 5.8 %collective-permute-start.54 = (f32[128,128]{1,0:T(8,128)S(1)}, f32[128,128]{1,0:T(8,128)S(1)}, u32[]{:S(2)}, u32[]{:S(2)}) collective-permute-start(f32[128,128]{1,0:T(8,128)S(1)} %add_add_fusion.refs_0_), channel_id=1, source_target_pairs={{0,16},{8,24},{16,0},{24,8},{32,48},{40,56},{48,32},{56,40},{64,80... | collective-permute-start | bytes 196616 | tf_op jit(solution)/shard_map/ppermute | solution.py:35
  288.3 5.5 %collective-permute-start.53 = (f32[128,128]{1,0:T(8,128)S(1)}, f32[128,128]{1,0:T(8,128)S(1)}, u32[]{:S(2)}, u32[]{:S(2)}) collective-permute-start(f32[128,128]{1,0:T(8,128)S(1)} %add_add_fusion.refs_0_), channel_id=1, source_target_pairs={{0,8},{8,16},{16,24},{24,0},{32,40},{40,48},{48,56},{56,32},{64,72... | collective-permute-start | bytes 196616 | tf_op jit(solution)/shard_map/ppermute | solution.py:35
  329.7 5.8 %collective-permute-start.58 = (f32[136,128]{1,0:T(8,128)S(1)}, f32[136,128]{1,0:T(8,128)S(1)}, u32[]{:S(2)}, u32[]{:S(2)}) collective-permute-start(f32[136,128]{1,0:T(8,128)S(1)} %shard_map.101.first), channel_id=1, source_target_pairs={{0,4},{1,5},{2,6},{3,7},{4,0},{5,1},{6,2},{7,3},{8,12},{9,13},{10,... | collective-permute-start | bytes 208904 | tf_op jit(solution)/shard_map/ppermute | solution.py:42
  330.6 5.7 %collective-permute-start.57 = (f32[136,128]{1,0:T(8,128)S(1)}, f32[136,128]{1,0:T(8,128)S(1)}, u32[]{:S(2)}, u32[]{:S(2)}) collective-permute-start(f32[136,128]{1,0:T(8,128)S(1)} %shard_map.101.first), channel_id=1, source_target_pairs={{0,2},{1,3},{2,4},{3,5},{4,6},{5,7},{6,0},{7,1},{8,10},{9,11},{10,... | collective-permute-start | bytes 208904 | tf_op jit(solution)/shard_map/ppermute | solution.py:42
  (19 other events, 83.4 us)
